TPU v7x, 32 devices: a whole 2x2x4 slice. The times are simulated.
32 devices in a mesh: seq: 8 (over z, x), exp: 4 (over y, core).
Axes of the slice: x: 2, y: 2, z: 4, core: 2. Of those that a mesh axis runs over, the one named last changes fastest.
Arguments:
- residual: bfloat16 [4096, 8192], P('seq', 'exp'), may hold values from -16 to 16
- queries: bfloat16 [4096, 4096], P('seq', 'exp'), may hold values from -6 to 6
- keys: bfloat16 [4096, 4096], P('seq', 'exp'), may hold values from -10 to 10
- values: bfloat16 [4096, 4096], P('seq', 'exp'), may hold values from -6 to 6
- documents: int32 [4096], replicated, may hold values from 0 to 1, as said below
- out_proj: bfloat16 [4096, 8192], P(None, 'exp'), may hold values from -0.09375 to 0.09375
- modality: int32 [4096], P('seq'), may hold values from 0 to 1, as said below
- norm_gain: float32 [2, 8192], P(None, 'exp'), may hold values from 0.25 to 1.75
- picks: int32 [4, 64], replicated, may hold values from 0 to 4095, as said below
- router: bfloat16 [8192, 4], P(None, 'exp'), may hold values from -0.0625 to 0.0625
- w_gate: bfloat16 [4, 8192, 4096], P('exp', None, 'seq'), may hold values from -0.0625 to 0.0625
- w_up: bfloat16 [4, 8192, 4096], P('exp', None, 'seq'), may hold values from -0.0625 to 0.0625
- w_down: bfloat16 [4, 4096, 8192], P('exp', 'seq'), may hold values from -0.09375 to 0.09375
Outputs:
- layer_out: bfloat16 [4096, 8192], P('seq', 'exp')
Inputs may be any that keep to these rules, and one draw needn't show every extreme that they name: `modality`: 0 marks a text token, 1 an image token. `documents`: 0 for the first document, 1 for the second; the second begins between position 1024 and 3072. `picks`: row e lists 64 different positions in ascending order; all carry modality 0 for e < 2 and modality 1 otherwise. Within each aligned block of 512 positions (the tokens of one index of seq) a row lists at most 16 positions, and every row lists exactly 16 in some block.
All inputs are finite; a program needn't handle non-finite values.
Results may differ from a plain program's by a relative error of at most 0.0035.
Values may be sent and summed in bfloat16 or wider, within the bound.
A program may use at most 128 MiB of HBM per device.

v0:
```python
import functools
import math

import jax
import jax.numpy as jnp
from jax import lax
from jax.experimental import pallas as pl
from jax.experimental.pallas import tpu as pltpu
from jax.sharding import PartitionSpec as P

D = 8192
HD = 128


block_rows = 512


MESH = pl.DeviceIdType.MESH


def greet(peers):
    barrier = pltpu.get_barrier_semaphore()
    for peer in peers:
        pl.semaphore_signal(barrier, inc=1, device_id=peer, device_id_type=MESH)
    pl.semaphore_wait(barrier, len(peers))


def cut(start, size):
    return pl.ds(pl.multiple_of(start, size), size)


def heads_out_kernel(n, width, q_ref, k_ref, v_ref, qo, ko, vo, send, recv, own):
    me = lax.axis_index("seq")
    tokens = q_ref.shape[0]
    greet([{"seq": lax.rem(me + i, n)} for i in range(1, n)])
    pairs = ((k_ref, ko), (v_ref, vo), (q_ref, qo))
    copies = []
    for i in range(1, n):
        to = lax.rem(me + i, n)
        for t, (src, dst) in enumerate(pairs):
            copies.append(
                pltpu.make_async_remote_copy(
                    src_ref=src.at[:, cut(to * width, width)],
                    dst_ref=dst.at[cut(me * tokens, tokens), :],
                    send_sem=send.at[t * n + i],
                    recv_sem=recv.at[t * n + i],
                    device_id={"seq": to},
                    device_id_type=MESH,
                )
            )
            copies[-1].start()
    for t, (src, dst) in enumerate(pairs):
        copies.append(
            pltpu.make_async_copy(
                src.at[:, cut(me * width, width)], dst.at[cut(me * tokens, tokens), :], own.at[t]
            )
        )
        copies[-1].start()
    for copy in copies:
        copy.wait()


def heads_out(queries, keys, values, n):
    tokens, columns = queries.shape
    width = columns // n
    whole = jax.ShapeDtypeStruct((n * tokens, width), queries.dtype)
    anywhere = pl.BlockSpec(memory_space=pl.ANY)
    return pl.pallas_call(
        functools.partial(heads_out_kernel, n, width),
        out_shape=(whole, whole, whole),
        in_specs=[anywhere] * 3,
        out_specs=(anywhere,) * 3,
        scratch_shapes=[
            pltpu.SemaphoreType.DMA((3 * n,)),
            pltpu.SemaphoreType.DMA((3 * n,)),
            pltpu.SemaphoreType.DMA((3,)),
        ],
        compiler_params=pltpu.CompilerParams(collective_id=0, has_side_effects=True),
    )(queries, keys, values)


def heads_back_kernel(n, ny, width, a_ref, o_ref, s_send, s_recv, y_send, y_recv, c_send, c_recv, own):
    me = lax.axis_index("seq")
    place = lax.axis_index("exp")
    y, core = place // 2, lax.rem(place, 2)
    sibling = {"exp": y * 2 + 1 - core}
    across = [{"exp": lax.rem(y + k, ny) * 2 + core} for k in range(1, ny)]
    tokens = o_ref.shape[0]
    span = n * width
    greet([{"seq": lax.rem(me + i, n)} for i in range(1, n)] + across + [sibling])

    def piece(exp_at, seq_at):
        return o_ref.at[:, cut(exp_at * span + seq_at * width, width)]

    local = pltpu.make_async_copy(a_ref.at[cut(me * tokens, tokens), :], piece(place, me), own)
    local.start()
    first = []
    for i in range(1, n):
        to = lax.rem(me + i, n)
        first.append(
            push(
                a_ref.at[cut(to * tokens, tokens), :],
                piece(place, me),
                s_send.at[i],
                s_recv.at[i],
                {"seq": to},
            )
        )
    second = []
    third = []
    for i in range(n):
        if i == 0:
            local.wait()
        else:
            first[i - 1].wait_recv()
        part = piece(place, lax.rem(me + n - i, n))
        for k in range(1, ny):
            at = i * ny + k
            second.append(push(part, part, y_send.at[at], y_recv.at[at], across[k - 1]))
        third.append(push(part, part, c_send.at[i * ny], c_recv.at[i * ny], sibling))
    for i in range(n):
        for k in range(1, ny):
            second[i * (ny - 1) + k - 1].wait_recv()
            at = i * ny + k
            part = piece(lax.rem(y + ny - k, ny) * 2 + core, lax.rem(me + n - i, n))
            third.append(push(part, part, c_send.at[at], c_recv.at[at], sibling))
    for copy in third:
        copy.wait_recv()
    for copy in first + second + third:
        copy.wait_send()


def heads_back(attended, n, n_exp):
    rows, width = attended.shape
    ny = n_exp // 2
    anywhere = pl.BlockSpec(memory_space=pl.ANY)
    return pl.pallas_call(
        functools.partial(heads_back_kernel, n, ny, width),
        out_shape=jax.ShapeDtypeStruct((rows // n, n_exp * n * width), attended.dtype),
        in_specs=[anywhere],
        out_specs=anywhere,
        scratch_shapes=[
            pltpu.SemaphoreType.DMA((n,)),
            pltpu.SemaphoreType.DMA((n,)),
            pltpu.SemaphoreType.DMA((n * ny,)),
            pltpu.SemaphoreType.DMA((n * ny,)),
            pltpu.SemaphoreType.DMA((n * ny,)),
            pltpu.SemaphoreType.DMA((n * ny,)),
            pltpu.SemaphoreType.DMA(()),
        ],
        compiler_params=pltpu.CompilerParams(collective_id=1, has_side_effects=True),
    )(attended)


def push(src, dst, send, recv, peer):
    copy = pltpu.make_async_remote_copy(
        src_ref=src, dst_ref=dst, send_sem=send, recv_sem=recv, device_id=peer, device_id_type=MESH
    )
    copy.start()
    return copy


def lines(me, nz):
    z, x = me // 2, lax.rem(me, 2)
    along = [{"seq": lax.rem(z + k, nz) * 2 + x} for k in range(1, nz)]
    return z, x, along, {"seq": z * 2 + 1 - x}


def ring_device(pos, n):
    half = pos // (n // 2)
    return (1 - half) * pos * 2 + half * ((n - 1 - pos) * 2 + 1)


def rows_kernel(n, ne, cap, width, r_ref, o_ref, e_send, e_recv, s_send, s_recv, own):
    me = lax.axis_index("seq")
    place = lax.axis_index("exp")
    z, x = me // 2, lax.rem(me, 2)
    pos = (1 - x) * z + x * (n - 1 - z)
    ways = (1, n - 1)
    nexts = [{"seq": ring_device(lax.rem(pos + way, n), n)} for way in ways]
    others = [{"exp": lax.rem(place + i, ne)} for i in range(1, ne)]
    greet(others + nexts)

    def piece(seq_at, exp_at):
        return o_ref.at[cut(seq_at * cap, cap), cut(exp_at * width, width)]

    local = pltpu.make_async_copy(r_ref.at[cut(place * cap, cap), :], piece(me, place), own)
    local.start()
    first = []
    for i in range(1, ne):
        src = r_ref.at[cut(lax.rem(place + i, ne) * cap, cap), :]
        first.append(push(src, piece(me, place), e_send.at[i], e_recv.at[i], others[i - 1]))
    hops = {}
    for t in range(n // 2):
        for i in range(ne):
            if t == 0:
                local.wait() if i == 0 else first[i - 1].wait_recv()
            for d in range(2):
                if t:
                    hops[i, d, t - 1].wait_recv()
                if t == n // 2 - 1 and i % 2 != d:
                    continue
                seq_at = ring_device(lax.rem(pos + n + t * (ways[1 - d]), n), n)
                part = piece(seq_at, lax.rem(place + ne - i, ne))
                at = (i * 2 + d) * (n // 2) + t
                hops[i, d, t] = push(part, part, s_send.at[at], s_recv.at[at], nexts[d])
    for i in range(ne):
        hops[i, i % 2, n // 2 - 1].wait_recv()
    for copy in first + list(hops.values()):
        copy.wait_send()


def share_rows(rows, n, ne):
    cap, width = rows.shape[0] // ne, rows.shape[1]
    anywhere = pl.BlockSpec(memory_space=pl.ANY)
    return pl.pallas_call(
        functools.partial(rows_kernel, n, ne, cap, width),
        out_shape=jax.ShapeDtypeStruct((n * cap, ne * width), rows.dtype),
        in_specs=[anywhere],
        out_specs=anywhere,
        scratch_shapes=[pltpu.SemaphoreType.DMA((ne,))] * 2
        + [pltpu.SemaphoreType.DMA((ne * n,))] * 2
        + [pltpu.SemaphoreType.DMA(())],
        compiler_params=pltpu.CompilerParams(collective_id=2, has_side_effects=True),
    )(rows)


def sums_kernel(
    nz, ne, cap, p_ref, g_ref, o_ref, x_buf, s_buf, z_buf, total, w_buf,
    x_send, x_recv, z_send, z_recv, e_send, e_recv, own,
):
    me = lax.axis_index("seq")
    z, x, along, partner = lines(me, nz)
    place = lax.axis_index("exp")
    others = [{"exp": lax.rem(place + i, ne)} for i in range(1, ne)]
    greet(along + [partner] + others)

    def rows_of(k, side):
        return cut((lax.rem(z + k, nz) * 2 + side) * cap, cap)

    order = list(range(1, nz)) + [0]
    pairs = {}
    for k in order:
        pairs[k] = push(p_ref.at[rows_of(k, 1 - x), :], x_buf.at[k], x_send.at[k], x_recv.at[k], partner)
    sent = []
    for k in order:
        pairs[k].wait_recv()
        both = p_ref[rows_of(k, x), :].astype(jnp.float32) + x_buf[k].astype(jnp.float32)
        if k:
            s_buf[k] = both.astype(jnp.bfloat16)
            sent.append(push(s_buf.at[k], z_buf.at[k], z_send.at[k], z_recv.at[k], along[k - 1]))
        else:
            total[...] = both
    for k in range(1, nz):
        sent[k - 1].wait_recv()
        total[...] += z_buf[k].astype(jnp.float32)
    w_buf[...] = (g_ref[...] * total[...]).astype(jnp.bfloat16)
    width = w_buf.shape[1] // ne
    mine = o_ref.at[cut(place * cap, cap), :]
    local = pltpu.make_async_copy(w_buf.at[:, cut(place * width, width)], mine, own)
    local.start()
    spread = []
    for i in range(1, ne):
        src = w_buf.at[:, cut(lax.rem(place + i, ne) * width, width)]
        spread.append(push(src, mine, e_send.at[i], e_recv.at[i], others[i - 1]))
    local.wait()
    for copy in spread:
        copy.wait_recv()
    for copy in list(pairs.values()) + sent + spread:
        copy.wait_send()


def sum_rows(partial, gate, n, ne):
    cap, width = partial.shape[0] // n, partial.shape[1]
    nz = n // 2
    slots = pltpu.VMEM((nz, cap, width), jnp.bfloat16)
    return pl.pallas_call(
        functools.partial(sums_kernel, nz, ne, cap),
        out_shape=jax.ShapeDtypeStruct((ne * cap, width // ne), jnp.bfloat16),
        in_specs=[pl.BlockSpec(memory_space=pltpu.VMEM)] * 2,
        out_specs=pl.BlockSpec(memory_space=pl.ANY),
        scratch_shapes=[slots, slots, slots]
        + [pltpu.VMEM((cap, width), jnp.float32), pltpu.VMEM((cap, width), jnp.bfloat16)]
        + [pltpu.SemaphoreType.DMA((nz,))] * 4
        + [pltpu.SemaphoreType.DMA((ne,))] * 2
        + [pltpu.SemaphoreType.DMA(())],
        compiler_params=pltpu.CompilerParams(collective_id=3, has_side_effects=True),
    )(partial, gate)


def flash_kernel(block, border_ref, q_ref, k_ref, v_ref, o_ref):
    at = pl.program_id(1)
    border = border_ref[0]
    q_start = at * block
    rows = q_start + lax.broadcasted_iota(jnp.int32, (block, 1), 0)
    low = jnp.where(rows >= border, border, 0)
    steps = lax.broadcasted_iota(jnp.int32, (block, block), 1)
    q = q_ref[...]
    scale = math.log2(math.e) / math.sqrt(HD)

    def scored(j):
        start = pl.multiple_of(j * block, block)
        s = lax.dot_general(
            q, k_ref[pl.ds(start, block), :], (((1,), (1,)), ((), ())), preferred_element_type=jnp.float32
        )
        return s * scale, start

    def mix(p, start):
        return jnp.dot(
            p.astype(jnp.bfloat16), v_ref[pl.ds(start, block), :], preferred_element_type=jnp.float32
        )

    s, start = scored(at)
    s = jnp.where((steps >= low - start) & (steps <= rows - start), s, -jnp.inf)
    top = jnp.max(s, axis=1, keepdims=True)
    p = jnp.exp2(s - top)
    state = (top, jnp.sum(p, axis=1, keepdims=True), mix(p, start))

    def step(j, state):
        top, total, out = state
        s, start = scored(j)
        s = jnp.where(steps >= low - start, s, -jnp.inf)
        new_top = jnp.maximum(top, jnp.max(s, axis=1, keepdims=True))
        factor = jnp.exp2(top - new_top)
        p = jnp.exp2(s - new_top)
        return (
            new_top,
            total * factor + jnp.sum(p, axis=1, keepdims=True),
            out * factor + mix(p, start),
        )

    begin = jnp.where(q_start >= border, border // block, 0)
    top, total, out = lax.fori_loop(begin, at, step, state)
    o_ref[...] = (out / total).astype(o_ref.dtype)


def flash(queries, keys, values, border):
    rows, width = queries.shape
    block = block_rows
    return pl.pallas_call(
        functools.partial(flash_kernel, block),
        out_shape=jax.ShapeDtypeStruct((rows, width), queries.dtype),
        grid_spec=pltpu.PrefetchScalarGridSpec(
            num_scalar_prefetch=1,
            grid=(width // HD, rows // block),
            in_specs=[
                pl.BlockSpec((block, HD), lambda h, i, b: (i, h)),
                pl.BlockSpec((rows, HD), lambda h, i, b: (0, h)),
                pl.BlockSpec((rows, HD), lambda h, i, b: (0, h)),
            ],
            out_specs=pl.BlockSpec((block, HD), lambda h, i, b: (i, h)),
        ),
    )(border, queries, keys, values)


def attend_by_head(queries, keys, values, documents, n, n_exp):
    border = jnp.sum((documents == 0).astype(jnp.int32)).reshape(1)
    q_all, k_all, v_all = heads_out(queries, keys, values, n)
    return heads_back(flash(q_all, k_all, v_all, border), n, n_exp)


def attend_by_token(queries, keys, values, documents):
    tokens = queries.shape[0]
    heads_here = queries.shape[1] // HD
    seq_pos = lax.axis_index("seq")
    start_row = seq_pos * tokens
    query_pos = start_row + jnp.arange(tokens, dtype=jnp.int32)
    query_doc = lax.dynamic_slice_in_dim(documents, start_row, tokens, 0)
    query_heads = queries.reshape(tokens, heads_here, HD)
    score_scale = 1.0 / math.sqrt(HD)

    def attend(state, key_rows, value_rows, key_start):
        row_count = key_rows.shape[0]
        key_pos = key_start + jnp.arange(row_count, dtype=jnp.int32)
        key_doc = lax.dynamic_slice_in_dim(documents, key_start, row_count, 0)
        scores = (
            jnp.einsum(
                "qhd,khd->qhk",
                query_heads,
                key_rows.reshape(row_count, heads_here, HD),
                preferred_element_type=jnp.float32,
            )
            * score_scale
        )
        allowed = (key_pos[None, :] <= query_pos[:, None]) & (
            key_doc[None, :] == query_doc[:, None]
        )
        scores = jnp.where(allowed[:, None, :], scores, -jnp.inf)
        running_max, running_sum, running_out = state
        new_max = jnp.maximum(running_max, jnp.max(scores, axis=2))
        factor = jnp.exp(running_max - new_max)
        weights = jnp.exp(scores - new_max[:, :, None])
        running_sum = running_sum * factor + jnp.sum(weights, axis=2)
        running_out = running_out * factor[:, :, None] + jnp.einsum(
            "qhk,khd->qhd",
            weights.astype(jnp.bfloat16),
            value_rows.reshape(row_count, heads_here, HD),
            preferred_element_type=jnp.float32,
        )
        return (new_max, running_sum, running_out)

    def visit_block(state, key_rows, value_rows, key_start):
        row_count = key_rows.shape[0]
        last_doc = lax.dynamic_index_in_dim(documents, key_start + row_count - 1, 0, keepdims=False)
        beyond = (key_start > query_pos[tokens - 1]) | (last_doc < query_doc[0])
        return lax.cond(
            beyond,
            lambda inner_state: inner_state,
            lambda inner_state: attend(inner_state, key_rows, value_rows, key_start),
            state,
        )

    initial = (
        jnp.full((tokens, heads_here), -1e30, jnp.float32),
        jnp.zeros((tokens, heads_here), jnp.float32),
        jnp.zeros((tokens, heads_here, HD), jnp.float32),
    )
    state = initial
    key_piece = lax.all_gather(keys, "seq", axis=0, tiled=True)
    value_piece = lax.all_gather(values, "seq", axis=0, tiled=True)
    row_count = key_piece.shape[0]
    blocks = row_count // block_rows
    key_stack = key_piece.reshape(blocks, block_rows, key_piece.shape[1])
    value_stack = value_piece.reshape(blocks, block_rows, value_piece.shape[1])

    def scan_step(inner_state, block_item):
        block_index, key_rows, value_rows = block_item
        return (visit_block(inner_state, key_rows, value_rows, block_index * block_rows), None)

    state, unused = lax.scan(
        scan_step, state, (jnp.arange(blocks, dtype=jnp.int32), key_stack, value_stack)
    )
    running_max, running_sum, running_out = state
    attended = (
        (running_out / running_sum[:, :, None])
        .reshape(tokens, heads_here * HD)
        .astype(jnp.bfloat16)
    )
    return lax.all_gather(attended, "exp", axis=1, tiled=True)


def shards(
    residual,
    queries,
    keys,
    values,
    documents,
    out_proj,
    modality,
    norm_gain,
    picks,
    router,
    w_gate,
    w_up,
    w_down,
):
    tokens = queries.shape[0]
    seq_pos = lax.axis_index("seq")
    start_row = seq_pos * tokens
    n_seq, n_exp = lax.axis_size("seq"), lax.axis_size("exp")
    if (queries.shape[1] // HD) % n_seq == 0 and n_exp % 2 == 0:
        attended = attend_by_head(queries, keys, values, documents, n_seq, n_exp)
    else:
        attended = attend_by_token(queries, keys, values, documents)
    mixed = jnp.dot(
        attended,
        out_proj,
        preferred_element_type=jnp.float32,
    )
    hidden_state = (residual.astype(jnp.float32) + mixed).astype(jnp.bfloat16)
    hidden_wide = hidden_state.astype(jnp.float32)
    square_total = lax.psum(jnp.sum(hidden_wide * hidden_wide, axis=1), "exp")
    inverse = lax.rsqrt(square_total / D + 1e-05)
    gain_rows = jnp.where(modality[:, None] == 0, norm_gain[0][None, :], norm_gain[1][None, :])
    normed = (hidden_wide * inverse[:, None] * gain_rows).astype(jnp.bfloat16)
    capacity = tokens // 32
    inside = (picks >= start_row) & (picks < start_row + tokens)
    slot_index = jnp.cumsum(inside.astype(jnp.int32), axis=1) - 1
    matched = inside[:, None, :] & (
        slot_index[:, None, :] == jnp.arange(capacity, dtype=jnp.int32)[None, :, None]
    )
    local_index = jnp.sum(jnp.where(matched, picks[:, None, :] - start_row, 0), axis=2)
    filled = jnp.any(matched, axis=2)
    rows_out = jnp.take(normed, local_index.reshape(-1), axis=0)
    rows_out = jnp.where(filled.reshape(-1, 1), rows_out, jnp.zeros_like(rows_out))
    piece = share_rows(rows_out, n_seq, n_exp)
    expert_rows = lax.dynamic_slice_in_dim(piece, seq_pos * capacity, capacity, 0)
    logits = jnp.dot(expert_rows, router, preferred_element_type=jnp.float32)[:, 0]
    gate_part = jnp.dot(piece, w_gate[0], preferred_element_type=jnp.float32)
    up_part = jnp.dot(piece, w_up[0], preferred_element_type=jnp.float32)
    inner_act = (jax.nn.silu(gate_part) * up_part).astype(jnp.bfloat16)
    partial = jnp.dot(inner_act, w_down[0], preferred_element_type=jnp.float32).astype(jnp.bfloat16)
    returned = sum_rows(partial, jax.nn.sigmoid(logits)[:, None], n_seq, n_exp)
    placing = (
        (jnp.arange(tokens, dtype=jnp.int32)[:, None] == local_index.reshape(1, -1))
        & filled.reshape(1, -1)
    ).astype(jnp.bfloat16)
    expert_add = jnp.dot(placing, returned, preferred_element_type=jnp.float32)
    return (hidden_wide + expert_add).astype(jnp.bfloat16)


def solution(mesh):
    return jax.shard_map(
        shards,
        mesh=mesh,
        in_specs=(
            P("seq", "exp"),
            P("seq", "exp"),
            P("seq", "exp"),
            P("seq", "exp"),
            P(),
            P(None, "exp"),
            P("seq"),
            P(None, "exp"),
            P(),
            P(None, "exp"),
            P("exp", None, "seq"),
            P("exp", None, "seq"),
            P("exp", "seq", None),
        ),
        out_specs=P("seq", "exp"),
        check_vma=False,
    )
```

profile of v0, /device:TPU:5, one launch (start us, length us, event | category | flops | bytes accessed | tf_op | source)
XLA Modules:
  0.0 250.8 jit_solution(14878014823164839420)
XLA Ops:
  0.0 0.0 copy-start
  0.0 0.7 fusion.38
  0.7 0.2 reduce_window_sum.11
  0.9 0.7 broadcast_add_fusion
  1.6 0.1 select_reduce_fusion
  1.8 0.1 reshape.70
  1.9 55.1 %shard_map.127 = (bf16[4096,128]{1,0:T(8,128)(2,1)}, bf16[4096,128]{1,0:T(8,128)(2,1)}, bf16[4096,128]{1,0:T(8,128)(2,1)}) custom-call(bf16[512,1024]{1,0:T(8,128)(2,1)} %q_ref.1, bf16[512,1024]{1,0:T(8,128)(2,1)} %k_ref.1, bf16[512,1024]{1,0:T(8,128)(2,1)} %v_ref.1), custom_call_target="tpu_custom_call" | custom-call | tf_op jit(solution)/shard_map/pallas_call | solution.py:68
  56.9 1.3 convert_reduce_fusion
  58.3 22.5 %shard_map.128.a_ref = bf16[4096,128]{1,0:T(8,128)(2,1)} custom-call(s32[1]{0:T(128)} %bitcast.border_ref, bf16[4096,128]{1,0:T(8,128)(2,1)} %get-tuple-element.8.q_ref, bf16[4096,128]{1,0:T(8,128)(2,1)} %get-tuple-element.9.k_ref, bf16[4096,128]{1,0:T(8,128)(2,1)} %get-tuple-element.10.v_ref), custom_call_target="tpu_custom_call" | custom-call | tf_op jit(solution)/shard_map/pallas_call | solution.py:340
  80.8 52.9 %shard_map.129 = bf16[512,4096]{1,0:T(8,128)(2,1)} custom-call(bf16[4096,128]{1,0:T(8,128)(2,1)} %shard_map.128.a_ref), custom_call_target="tpu_custom_call" | custom-call | tf_op jit(solution)/shard_map/pallas_call | solution.py:137
  133.7 0.0 copy-start.3
  133.7 0.0 copy-start.4
  133.7 14.2 %fusion.5 = (f32[512]{0:T(512)S(1)}, bf16[512,2048]{1,0:T(8,128)(2,1)S(1)}) fusion(bf16[512,4096]{1,0:T(8,128)(2,1)} %shard_map.129, bf16[4096,2048]{1,0:T(8,128)(2,1)} %param.18, bf16[512,2048]{1,0:T(8,128)(2,1)} %param.13), kind=kOutput, calls=%fused_computation.10 | convolution fusion | flops 8596226048 | bytes 25167872 | tf_op jit(solution)/shard_map/dot_general | solution.py:465
  147.9 0.0 copy-start.2
  147.9 6.2 %psum.7 = f32[512]{0:T(512)S(1)} all-reduce(f32[512]{0:T(512)S(1)} %get-tuple-element.15), channel_id=1, replica_groups=mesh['seq'=8,'exp'=4] {'exp'}, use_global_device_ids=true, to_apply=%region_5.6 | all-reduce | flops 512 | bytes 4096 | tf_op jit(solution)/shard_map/psum | solution.py:472
  154.1 0.0 copy-done.3
  154.1 0.0 copy-done.4
  154.2 2.2 fusion.7
  156.3 2.8 %gather_fusion = bf16[64,2048]{1,0:T(8,128)(2,1)S(1)} fusion(bf16[512,2048]{1,0:T(8,128)(2,1)} %fusion.7, s32[1024]{0:T(1024)S(1)} %pad_clamp_fusion), kind=kCustom, calls=%fused_computation | custom fusion | bytes 524544 | tf_op jit(solution)/shard_map/jit(_take)/gather | solution.py:484
  159.2 0.1 eq.47
  159.3 0.1 fusion.34
  159.4 0.1 and.32
  159.5 0.8 select_select_fusion.r_ref
  160.3 0.0 copy-done.2
  160.4 31.3 %shard_map.130 = bf16[128,8192]{1,0:T(8,128)(2,1)} custom-call(bf16[64,2048]{1,0:T(8,128)(2,1)} %select_select_fusion.r_ref), custom_call_target="tpu_custom_call" | custom-call | tf_op jit(solution)/shard_map/pallas_call | solution.py:216
  191.7 5.4 %fusion.3 = f32[128,512]{1,0:T(8,128)S(1)} fusion(bf16[128,8192]{1,0:T(8,128)(2,1)} %shard_map.130, bf16[1,8192,512]{2,1,0:T(8,128)(2,1)} %param.23), kind=kOutput, calls=%fused_computation.5 | convolution fusion | flops 1073741824 | bytes 10747904 | tf_op jit(solution)/shard_map/dot_general | solution.py:489
  197.1 9.6 %convolution_convert_fusion.p_ref = bf16[128,8192]{1,0:T(8,128)(2,1)} fusion(bf16[1,512,8192]{2,1,0:T(8,128)(2,1)} %param.25, bf16[128,8192]{1,0:T(8,128)(2,1)S(1)} %copy-done.1, bf16[1,8192,512]{2,1,0:T(8,128)(2,1)} %param.24, f32[128,512]{1,0:T(8,128)S(1)} %fusion.3), kind=kOutput, calls=%fused_computation.1 | convolution fusion | flops 2148925440 | bytes 21233664 | tf_op jit(solution)/shard_map/dot_general | solution.py:492
  206.7 0.0 copy-done
  206.7 0.2 fusion.19
  206.9 0.7 copy.15.g_ref
  207.6 39.4 %shard_map.131 = bf16[64,2048]{1,0:T(8,128)(2,1)} custom-call(bf16[128,8192]{1,0:T(8,128)(2,1)} %convolution_convert_fusion.p_ref, f32[16,1]{1,0:T(8,128)} %copy.15.g_ref), custom_call_target="tpu_custom_call" | custom-call | tf_op jit(solution)/shard_map/pallas_call | solution.py:277
  247.0 3.7 %fusion.8 = bf16[512,2048]{1,0:T(8,128)(2,1)} fusion(bf16[512,2048]{1,0:T(8,128)(2,1)} %copy-done.2, bf16[64,2048]{1,0:T(8,128)(2,1)} %shard_map.131, s32[64]{0:T(128)S(1)} %eq.47, pred[64]{0:T(512)(128)(4,1)S(1)} %and.32), kind=kOutput, calls=%fused_computation.13 | convolution fusion | flops 137428992 | bytes 4456768 | tf_op jit(solution)/shard_map/dot_general | solution.py:498
  (8 shorter events, 0.1 us)
Async XLA Ops:
  0.0 206.7 %copy-start = (bf16[8192,1]{0,1:T(2,128)(2,1)S(1)}, bf16[8192,1]{0,1:T(2,128)(2,1)}, u32[]{:S(2)}) copy-start(bf16[8192,1]{0,1:T(2,128)(2,1)} %param.22) | copy-start | bytes 49156
  133.7 20.4 %copy-start.3 = (f32[2,2048]{1,0:T(2,128)S(1)}, f32[2,2048]{1,0:T(2,128)}, u32[]{:S(2)}) copy-start(f32[2,2048]{1,0:T(2,128)} %param.20) | copy-start | bytes 49156
  133.7 20.4 %copy-start.4 = (s32[512]{0:T(512)S(1)}, s32[512]{0:T(512)}, u32[]{:S(2)}) copy-start(s32[512]{0:T(512)} %param.19) | copy-start | bytes 6148
  147.9 12.5 %copy-start.2 = (bf16[512,2048]{1,0:T(8,128)(2,1)}, bf16[512,2048]{1,0:T(8,128)(2,1)S(1)}, u32[]{:S(2)}) copy-start(bf16[512,2048]{1,0:T(8,128)(2,1)S(1)} %get-tuple-element.16) | copy-start | bytes 6291460
  191.7 5.4 %copy-start.1 = (bf16[128,8192]{1,0:T(8,128)(2,1)S(1)}, bf16[128,8192]{1,0:T(8,128)(2,1)}, u32[]{:S(2)}) copy-start(bf16[128,8192]{1,0:T(8,128)(2,1)} %shard_map.130) | copy-start | bytes 6291460
where the time goes:
time: 255 us; the launch traced here: 251 us
  Pallas kernels  201 us (79%)
  matrix products  33.1 us (13%)
  other arithmetic  6.28 us (2%)
  blocking collectives  6.23 us (2%)
  local copies, waits for them, and re-layouts  3.85 us (2%)
    pallas_call x1, Pallas kernels, heads_out(): pl.pallas_call(functools.partial(heads_out_kernel, n, width), out_shape=(...  55.1 us
    pallas_call x1, Pallas kernels, heads_back(): pl.pallas_call(functools.partial(heads_back_kernel, n, ny, width), out_sh...  52.9 us
    pallas_call x1, Pallas kernels, sum_rows(): pl.pallas_call(functools.partial(sums_kernel, nz, ne, cap), out_shape=jax...  39.4 us
    pallas_call x1, Pallas kernels, share_rows(): pl.pallas_call(functools.partial(rows_kernel, n, ne, cap, width), out_sha...  31.3 us
    pallas_call x1, Pallas kernels, flash(): pl.pallas_call(functools.partial(flash_kernel, block), out_shape=jax.Shap...  22.5 us
    dot_general x1, matrix products, shards(): mixed = jnp.dot(attended, out_proj, preferred_element_type=jnp.float32)  14.2 us
    dot_general x1, matrix products, shards(): jnp.dot(inner_act, w_down[0], preferred_element_type=jnp.float32)  9.61 us
    psum x1, blocking collectives, shards(): square_total = lax.psum(jnp.sum(hidden_wide * hidden_wide, axis=1), 'exp')  6.23 us

commit v1 on v0

--- a/solution.py
+++ b/solution.py
@@ -359,6 +359,365 @@
     return heads_back(flash(q_all, k_all, v_all, border), n, n_exp)
 
 
+def chain_kernel(
+    nz, ne, group, causal_span, border_ref, q_ref, k_ref, v_ref, o_ref,
+    q0, q1, q2, kb, vb, o0, o1, c0, c1, s2, s1, p2, p1, ls2, ls1, lp2, lp1, fin, back,
+    load, x_send, x_recv, d0_send, d0_recv, d1_send, d1_recv, u2_send, u2_recv, g2_send, g2_recv,
+    u1_send, u1_recv, g1_send, g1_recv, b_send, b_recv, y_send, y_recv, m_send, m_recv,
+    r_send, r_recv, own,
+):
+    me = lax.axis_index("seq")
+    place = lax.axis_index("exp")
+    z, x = me // 2, lax.rem(me, 2)
+    y, core = place // 2, lax.rem(place, 2)
+    ny = ne // 2
+    tokens = q_ref.shape[0]
+    steps = 2 * group
+    up = {"seq": lax.rem(z + 1, nz) * 2 + x}
+    down = {"seq": lax.rem(z + nz - 1, nz) * 2 + x}
+    partner = {"seq": z * 2 + 1 - x}
+    sibling = {"exp": y * 2 + 1 - core}
+    far_place = lax.rem(y + 1, ny) * 2 + core
+    far = {"exp": far_place}
+    has1, has2, low1 = z + 1 < nz, z + 2 < nz, z >= 1
+    border = border_ref[0]
+    scale = math.log2(math.e) / math.sqrt(HD)
+    greet([up, down, partner, sibling, far])
+
+    def remote(src, dst, send, recv, peer):
+        return pltpu.make_async_remote_copy(
+            src_ref=src, dst_ref=dst, send_sem=send, recv_sem=recv, device_id=peer, device_id_type=MESH
+        )
+
+    def half(ref, h, side):
+        return ref.at[h, cut(side * tokens, tokens), :]
+
+    def columns(ref, h, side):
+        return ref.at[:, cut((side * group + h) * HD, HD)]
+
+    def loads(h):
+        return (
+            pltpu.make_async_copy(columns(q_ref, h, x), q0.at[2 * h], load.at[3 * h]),
+            pltpu.make_async_copy(columns(k_ref, h, x), half(kb, h, x), load.at[3 * h + 1]),
+            pltpu.make_async_copy(columns(v_ref, h, x), half(vb, h, x), load.at[3 * h + 2]),
+        )
+
+    def swaps(h):
+        side = 1 - x
+        return tuple(
+            remote(columns(src, h, side), dst, x_send.at[3 * h + t], x_recv.at[3 * h + t], partner)
+            for t, (src, dst) in enumerate(
+                ((q_ref, q0.at[2 * h + 1]), (k_ref, half(kb, h, x)), (v_ref, half(vb, h, x)))
+            )
+        )
+
+    def q_down(t):
+        return remote(q0.at[t], q1.at[t], d0_send.at[t], d0_recv.at[t], down)
+
+    def q_further(t):
+        return remote(q1.at[t], q2.at[t], d1_send.at[t], d1_recv.at[t], down)
+
+    def part2_up(t):
+        return (
+            remote(s2.at[t], p2.at[t], u2_send.at[t], u2_recv.at[t], up),
+            remote(ls2.at[t], lp2.at[t], g2_send.at[t], g2_recv.at[t], up),
+        )
+
+    def part1_up(t):
+        return (
+            remote(s1.at[t], p1.at[t], u1_send.at[t], u1_recv.at[t], up),
+            remote(ls1.at[t], lp1.at[t], g1_send.at[t], g1_recv.at[t], up),
+        )
+
+    def give_back(t):
+        return remote(back.at[t // 2], fin.at[t], b_send.at[t // 2], b_recv.at[t // 2], partner)
+
+    def spot(at, t):
+        j = lax.rem(t, 2)
+        side = x + j * (1 - 2 * x)
+        return o_ref.at[:, cut(((at * 2 + side) * group + t // 2) * HD, HD)]
+
+    def keep(t):
+        return pltpu.make_async_copy(fin.at[t], spot(place, t), own.at[t])
+
+    def to_far(t):
+        return remote(fin.at[t], spot(place, t), y_send.at[t], y_recv.at[t], far)
+
+    def to_sibling(t):
+        return remote(fin.at[t], spot(place, t), m_send.at[t], m_recv.at[t], sibling)
+
+    def relay(t):
+        return remote(spot(far_place, t), spot(far_place, t), r_send.at[t], r_recv.at[t], sibling)
+
+    tile = HD
+    tiles = tokens // tile
+    span = kb.shape[1]
+    key_base = z * span
+    diagonal = lax.broadcasted_iota(jnp.int32, (tile, tile), 0) == lax.broadcasted_iota(
+        jnp.int32, (tile, tile), 1
+    )
+
+    def attend(q_of, h, level, t, put):
+        j = lax.rem(t, 2)
+        side = x + j * (1 - 2 * x)
+        base = ((z + level) * 2 + side) * tokens - key_base
+        edge = border - key_base
+        keys, vals = kb[h], vb[h]
+        at = lax.broadcasted_iota(jnp.int32, (tile, span), 1)
+        for r in range(tiles):
+            rows = base + r * tile + lax.broadcasted_iota(jnp.int32, (tile, 1), 0)
+            low = jnp.where(rows >= edge, edge, -key_base)
+            s = lax.dot_general(
+                q_of[r * tile : (r + 1) * tile, :], keys, (((1,), (1,)), ((), ())),
+                preferred_element_type=jnp.float32,
+            )
+            seen = at >= low
+            if level == 0:
+                seen = seen & (at <= rows)
+            s = jnp.where(seen, s, -1e30)
+            top = jnp.max(s, axis=1, keepdims=True) * scale
+            p = jnp.exp2(s * scale - top)
+            total = jnp.sum(p, axis=1, keepdims=True)
+            out = jnp.dot(p.astype(jnp.bfloat16), vals, preferred_element_type=jnp.float32)
+            put(r, out / total, top + jnp.log2(total))
+
+    def flat(level):
+        return jnp.sum(jnp.where(diagonal, level, 0.0), axis=0, keepdims=True)
+
+    def upright(ref, r):
+        return jnp.sum(jnp.where(diagonal, ref[r : r + 1, :], 0.0), axis=1, keepdims=True)
+
+    def joined(out, level, p_of, l_of, r):
+        other = upright(l_of, r)
+        top = jnp.maximum(level, other)
+        mine, theirs = jnp.exp2(level - top), jnp.exp2(other - top)
+        both = mine + theirs
+        out = (out * mine + p_of[r * tile : (r + 1) * tile, :].astype(jnp.float32) * theirs) / both
+        return out, top + jnp.log2(both)
+
+    for h in range(group):
+        for copy in swaps(h):
+            copy.start()
+        for copy in loads(h):
+            copy.start()
+
+    def send_own(t):
+        @pl.when(lax.rem(t, 2) == 0)
+        def _():
+            loads(t // 2)[0].wait()
+
+        @pl.when(lax.rem(t, 2) == 1)
+        def _():
+            swaps(t // 2)[0].wait_recv()
+
+        @pl.when(low1)
+        def _():
+            q_down(t).start()
+
+    def forward(t):
+        @pl.when(has1)
+        def _():
+            q_down(t).wait_recv()
+
+            @pl.when(low1)
+            def _():
+                q_further(t).start()
+
+    def spread(t):
+        keep(t).start()
+        to_far(t).start()
+        to_sibling(t).start()
+
+    send_own(jnp.int32(0))
+    send_own(jnp.int32(1))
+    forward(jnp.int32(0))
+
+    def step(i, carry):
+        live = i < steps
+
+        @pl.when(i + 2 < steps)
+        def _():
+            send_own(i + 2)
+
+        @pl.when(i + 1 < steps)
+        def _():
+            forward(i + 1)
+
+        @pl.when(live & (lax.rem(i, 2) == 0))
+        def _():
+            for copy in loads(i // 2)[1:]:
+                copy.wait()
+            for copy in swaps(i // 2)[1:]:
+                copy.wait_recv()
+
+        @pl.when(live & has2)
+        def _():
+            q_further(i).wait_recv()
+
+            def put(r, out, level):
+                s2[i, r * tile : (r + 1) * tile, :] = out.astype(jnp.bfloat16)
+                ls2[i, r : r + 1, :] = flat(level)
+
+            attend(q2.at[i], i // 2, 2, i, put)
+            for copy in part2_up(i):
+                copy.start()
+
+        t1 = i - 1
+
+        @pl.when((t1 >= 0) & (t1 < steps) & has1)
+        def _():
+            def put(r, out, level):
+                s1[t1, r * tile : (r + 1) * tile, :] = out.astype(jnp.bfloat16)
+                ls1[t1, r : r + 1, :] = flat(level)
+
+            @pl.when(low1)
+            def _():
+                for copy in part2_up(t1):
+                    copy.wait_recv()
+                for r in range(tiles):
+                    put(r, *joined(o1[t1, r * tile : (r + 1) * tile, :], c1[t1, r * tile : (r + 1) * tile, :], p2.at[t1], lp2.at[t1], r))
+
+            @pl.when(jnp.logical_not(low1))
+            def _():
+                for r in range(tiles):
+                    put(r, o1[t1, r * tile : (r + 1) * tile, :], c1[t1, r * tile : (r + 1) * tile, :])
+
+            for copy in part1_up(t1):
+                copy.start()
+
+        @pl.when(live & has1)
+        def _():
+            def put(r, out, level):
+                o1[i, r * tile : (r + 1) * tile, :] = out
+                c1[i, r * tile : (r + 1) * tile, :] = level
+
+            attend(q1.at[i], i // 2, 1, i, put)
+
+        t0 = i - 2
+
+        @pl.when((t0 >= 0) & (t0 < steps))
+        def _():
+            def finish(put):
+                @pl.when(low1)
+                def _():
+                    for copy in part1_up(t0):
+                        copy.wait_recv()
+                    for r in range(tiles):
+                        out, level = joined(o0[t0, r * tile : (r + 1) * tile, :], c0[t0, r * tile : (r + 1) * tile, :], p1.at[t0], lp1.at[t0], r)
+                        put(r, out)
+
+                @pl.when(jnp.logical_not(low1))
+                def _():
+                    for r in range(tiles):
+                        put(r, o0[t0, r * tile : (r + 1) * tile, :])
+
+            @pl.when(lax.rem(t0, 2) == 0)
+            def _():
+                def put(r, out):
+                    fin[t0, r * tile : (r + 1) * tile, :] = out.astype(jnp.bfloat16)
+
+                finish(put)
+                spread(t0)
+
+            @pl.when(lax.rem(t0, 2) == 1)
+            def _():
+                def put(r, out):
+                    back[t0 // 2, r * tile : (r + 1) * tile, :] = out.astype(jnp.bfloat16)
+
+                finish(put)
+                give_back(t0).start()
+
+        @pl.when(live)
+        def _():
+            def put(r, out, level):
+                o0[i, r * tile : (r + 1) * tile, :] = out
+                c0[i, r * tile : (r + 1) * tile, :] = level
+
+            attend(q0.at[i], i // 2, 0, i, put)
+
+        t4 = i - 3
+
+        @pl.when((t4 >= 0) & (t4 < steps) & (lax.rem(t4, 2) == 1))
+        def _():
+            give_back(t4).wait_recv()
+            spread(t4)
+
+        t5 = i - 5
+
+        @pl.when((t5 >= 0) & (t5 < steps))
+        def _():
+            to_far(t5).wait_recv()
+            relay(t5).start()
+
+        return carry
+
+    lax.fori_loop(0, steps + 5, step, 0)
+
+    def settle(t, carry):
+        to_sibling(t).wait_recv()
+        relay(t).wait_recv()
+        keep(t).wait()
+        to_far(t).wait_send()
+        to_sibling(t).wait_send()
+        relay(t).wait_send()
+
+        @pl.when(low1)
+        def _():
+            q_down(t).wait_send()
+
+            @pl.when(has1)
+            def _():
+                q_further(t).wait_send()
+
+        @pl.when(has1)
+        def _():
+            for copy in part1_up(t):
+                copy.wait_send()
+
+        @pl.when(has2)
+        def _():
+            for copy in part2_up(t):
+                copy.wait_send()
+
+        @pl.when(lax.rem(t, 2) == 1)
+        def _():
+            give_back(t).wait_send()
+            for copy in swaps(t // 2):
+                copy.wait_send()
+
+        return carry
+
+    lax.fori_loop(0, steps, settle, 0)
+
+
+def attend_by_chain(queries, keys, values, documents, n, n_exp):
+    tokens, width = queries.shape
+    group = width // HD // 2
+    steps = 2 * group
+    nz = n // 2
+    border = jnp.sum((documents == 0).astype(jnp.int32)).reshape(1)
+    anywhere = pl.BlockSpec(memory_space=pl.ANY)
+    bf, f32 = jnp.bfloat16, jnp.float32
+    chunks = pltpu.VMEM((steps, tokens, HD), bf)
+    side = pltpu.VMEM((group, 2 * tokens, HD), bf)
+    wide = pltpu.VMEM((steps, tokens, HD), f32)
+    thin = pltpu.VMEM((steps, tokens, 1), f32)
+    flats = pltpu.VMEM((steps, max(8, tokens // HD), HD), f32)
+    sems = lambda count: pltpu.SemaphoreType.DMA((count,))
+    return pl.pallas_call(
+        functools.partial(chain_kernel, nz, n_exp, group, None),
+        out_shape=jax.ShapeDtypeStruct((tokens, n_exp * width), queries.dtype),
+        in_specs=[pl.BlockSpec(memory_space=pltpu.SMEM)] + [anywhere] * 3,
+        out_specs=anywhere,
+        scratch_shapes=[chunks] * 3 + [side] * 2 + [wide] * 2 + [thin] * 2 + [chunks] * 4 + [flats] * 4
+        + [chunks, pltpu.VMEM((group, tokens, HD), bf)]
+        + [sems(3 * group)] * 3 + [sems(steps)] * 12 + [sems(group)] * 2 + [sems(steps)] * 6 + [sems(steps)],
+        compiler_params=pltpu.CompilerParams(
+            collective_id=0, has_side_effects=True, vmem_limit_bytes=48 * 1024 * 1024
+        ),
+    )(border, queries, keys, values)
+
+
 def attend_by_token(queries, keys, values, documents):
     tokens = queries.shape[0]
     heads_here = queries.shape[1] // HD
@@ -459,7 +818,7 @@
     start_row = seq_pos * tokens
     n_seq, n_exp = lax.axis_size("seq"), lax.axis_size("exp")
     if (queries.shape[1] // HD) % n_seq == 0 and n_exp % 2 == 0:
-        attended = attend_by_head(queries, keys, values, documents, n_seq, n_exp)
+        attended = attend_by_chain(queries, keys, values, documents, n_seq, n_exp)
     else:
         attended = attend_by_token(queries, keys, values, documents)
     mixed = jnp.dot(

time: 255 us -> 206 us (0.81)
  Pallas kernels: 201 us -> 150 us
  local copies, waits for them, and re-layouts: 3.85 us -> 7.53 us
    pallas_call x3 -> x1, Pallas kernels: 130 us -> 80 us  [attend_by_chain(): pl.pallas_call(functools.partial(chain_kernel, nz, n_exp, group, None), o...]
    unnamed x10 -> x18, local copies, waits for them, and re-layouts: 0.03 us -> 3.7 us
where the time goes in v1:
time: 206 us; the launch traced here: 202 us
  Pallas kernels  150 us (73%)
  matrix products  32.8 us (16%)
  local copies, waits for them, and re-layouts  7.53 us (4%)
  other arithmetic  6.31 us (3%)
  blocking collectives  5.35 us (3%)
    pallas_call x1, Pallas kernels, attend_by_chain(): pl.pallas_call(functools.partial(chain_kernel, nz, n_exp, group, None), o...  80 us
    pallas_call x1, Pallas kernels, sum_rows(): pl.pallas_call(functools.partial(sums_kernel, nz, ne, cap), out_shape=jax...  38.8 us
    pallas_call x1, Pallas kernels, share_rows(): pl.pallas_call(functools.partial(rows_kernel, n, ne, cap, width), out_sha...  31.3 us
    dot_general x1, matrix products, shards(): mixed = jnp.dot(attended, out_proj, preferred_element_type=jnp.float32)  13.9 us
    dot_general x1, matrix products, shards(): jnp.dot(inner_act, w_down[0], preferred_element_type=jnp.float32)  9.6 us
    dot_general x1, matrix products, shards(): gate_part = jnp.dot(piece, w_gate[0], preferred_element_type=jnp.float32)  5.42 us
    psum x1, blocking collectives, shards(): square_total = lax.psum(jnp.sum(hidden_wide * hidden_wide, axis=1), 'exp')  5.35 us

profile of v1, /device:TPU:5, one launch (start us, length us, event | category | flops | bytes accessed | tf_op | source)
XLA Modules:
  0.0 202.2 jit_solution(10656540910790584826)
XLA Ops:
  0.0 0.0 copy-start
  0.0 0.7 fusion.38
  0.7 0.2 reduce_window_sum.11
  0.9 0.7 broadcast_add_fusion
  1.6 0.1 select_reduce_fusion
  1.8 0.1 reshape.70
  1.9 1.4 convert_reduce_fusion
  3.2 1.2 copy-done.1
  4.5 1.2 copy-done.2
  5.7 1.2 copy-done.3
  6.9 80.0 %shard_map.127 = bf16[512,4096]{1,0:T(8,128)(2,1)} custom-call(s32[1]{0:T(128)} %bitcast.border_ref, bf16[512,1024]{1,0:T(8,128)(2,1)S(1)} %copy-done.1, bf16[512,1024]{1,0:T(8,128)(2,1)S(1)} %copy-done.2, bf16[512,1024]{1,0:T(8,128)(2,1)S(1)} %copy-done.3), custom_call_target="tpu_custom_call" | custom-call | tf_op jit(solution)/shard_map/pallas_call | solution.py:707
  87.0 0.0 copy-done.8
  87.0 0.0 copy-start.6
  87.0 0.0 copy-start.7
  87.0 13.9 %fusion.5 = (f32[512]{0:T(512)S(1)}, bf16[512,2048]{1,0:T(8,128)(2,1)S(1)}) fusion(bf16[512,4096]{1,0:T(8,128)(2,1)} %shard_map.127, bf16[4096,2048]{1,0:T(8,128)(2,1)} %param.18, bf16[512,2048]{1,0:T(8,128)(2,1)S(1)} %copy-done.8), kind=kOutput, calls=%fused_computation.10 | convolution fusion | flops 8596226048 | bytes 25167872 | tf_op jit(solution)/shard_map/dot_general | solution.py:824
  100.9 0.0 copy-start.5
  100.9 5.3 %psum.7 = f32[512]{0:T(512)S(1)} all-reduce(f32[512]{0:T(512)S(1)} %get-tuple-element.9), channel_id=1, replica_groups=mesh['seq'=8,'exp'=4] {'exp'}, use_global_device_ids=true, to_apply=%region_5.6 | all-reduce | flops 512 | bytes 4096 | tf_op jit(solution)/shard_map/psum | solution.py:831
  106.3 0.0 copy-done.6
  106.3 2.2 %fusion.7 = bf16[512,2048]{1,0:T(8,128)(2,1)} fusion(bf16[512,2048]{1,0:T(8,128)(2,1)S(1)} %get-tuple-element.10, f32[2048]{0:T(1024)S(1)} %bitcast.41, f32[2048]{0:T(1024)S(1)} %bitcast.40, f32[512]{0:T(512)S(1)} %add_rsqrt_fusion, pred[512]{0:T(512)(128)(4,1)S(1)} %broadcast_compare_fusion), kind=kLoop, calls=%fused_computation.12 | loop fusion | flops 5242880 | bytes 4213248 | tf_op jit(solution)/shard_map/convert_element_type | solution.py:834
  108.5 2.8 %gather_fusion = bf16[64,2048]{1,0:T(8,128)(2,1)S(1)} fusion(bf16[512,2048]{1,0:T(8,128)(2,1)} %fusion.7, s32[1024]{0:T(1024)S(1)} %pad_clamp_fusion), kind=kCustom, calls=%fused_computation | custom fusion | bytes 524544 | tf_op jit(solution)/shard_map/jit(_take)/gather | solution.py:843
  111.3 0.1 eq.47
  111.4 0.1 fusion.34
  111.6 0.1 and.32
  111.6 0.8 select_select_fusion.r_ref
  112.5 31.3 %shard_map.128 = bf16[128,8192]{1,0:T(8,128)(2,1)} custom-call(bf16[64,2048]{1,0:T(8,128)(2,1)} %select_select_fusion.r_ref), custom_call_target="tpu_custom_call" | custom-call | tf_op jit(solution)/shard_map/pallas_call | solution.py:216
  143.8 5.4 %fusion.3 = f32[128,512]{1,0:T(8,128)S(1)} fusion(bf16[128,8192]{1,0:T(8,128)(2,1)} %shard_map.128, bf16[1,8192,512]{2,1,0:T(8,128)(2,1)} %param.23), kind=kOutput, calls=%fused_computation.5 | convolution fusion | flops 1073741824 | bytes 10747904 | tf_op jit(solution)/shard_map/dot_general | solution.py:848
  149.2 9.6 %convolution_convert_fusion.p_ref = bf16[128,8192]{1,0:T(8,128)(2,1)} fusion(bf16[1,512,8192]{2,1,0:T(8,128)(2,1)} %param.25, bf16[128,8192]{1,0:T(8,128)(2,1)S(1)} %copy-done.4, bf16[1,8192,512]{2,1,0:T(8,128)(2,1)} %param.24, f32[128,512]{1,0:T(8,128)S(1)} %fusion.3), kind=kOutput, calls=%fused_computation.1 | convolution fusion | flops 2148925440 | bytes 21233664 | tf_op jit(solution)/shard_map/dot_general | solution.py:851
  158.8 0.0 copy-done
  158.8 0.2 fusion.19
  159.0 0.7 copy.15.g_ref
  159.7 38.8 %shard_map.129 = bf16[64,2048]{1,0:T(8,128)(2,1)} custom-call(bf16[128,8192]{1,0:T(8,128)(2,1)} %convolution_convert_fusion.p_ref, f32[16,1]{1,0:T(8,128)} %copy.15.g_ref), custom_call_target="tpu_custom_call" | custom-call | tf_op jit(solution)/shard_map/pallas_call | solution.py:277
  198.5 3.7 %fusion.8 = bf16[512,2048]{1,0:T(8,128)(2,1)} fusion(bf16[512,2048]{1,0:T(8,128)(2,1)} %copy-done.5, bf16[64,2048]{1,0:T(8,128)(2,1)} %shard_map.129, s32[64]{0:T(128)S(1)} %eq.47, pred[64]{0:T(512)(128)(4,1)S(1)} %and.32), kind=kOutput, calls=%fused_computation.13 | convolution fusion | flops 137428992 | bytes 4456768 | tf_op jit(solution)/shard_map/dot_general | solution.py:857
  (14 shorter events, 0.1 us)
Async XLA Ops:
  0.0 158.8 %copy-start = (bf16[8192,1]{0,1:T(2,128)(2,1)S(1)}, bf16[8192,1]{0,1:T(2,128)(2,1)}, u32[]{:S(2)}) copy-start(bf16[8192,1]{0,1:T(2,128)(2,1)} %param.22) | copy-start | bytes 49156
  3.2 1.2 copy-start.1
  4.5 1.2 copy-start.2
  5.7 1.2 copy-start.3
  6.9 80.0 %copy-start.8 = (bf16[512,2048]{1,0:T(8,128)(2,1)S(1)}, bf16[512,2048]{1,0:T(8,128)(2,1)}, u32[]{:S(2)}) copy-start(bf16[512,2048]{1,0:T(8,128)(2,1)} %param.13) | copy-start | bytes 6291460
  87.0 19.3 %copy-start.6 = (f32[2,2048]{1,0:T(2,128)S(1)}, f32[2,2048]{1,0:T(2,128)}, u32[]{:S(2)}) copy-start(f32[2,2048]{1,0:T(2,128)} %param.20) | copy-start | bytes 49156
  87.0 19.3 %copy-start.7 = (s32[512]{0:T(512)S(1)}, s32[512]{0:T(512)}, u32[]{:S(2)}) copy-start(s32[512]{0:T(512)} %param.19) | copy-start | bytes 6148
  100.9 11.6 %copy-start.5 = (bf16[512,2048]{1,0:T(8,128)(2,1)}, bf16[512,2048]{1,0:T(8,128)(2,1)S(1)}, u32[]{:S(2)}) copy-start(bf16[512,2048]{1,0:T(8,128)(2,1)S(1)} %get-tuple-element.10) | copy-start | bytes 6291460
  143.8 5.4 %copy-start.4 = (bf16[128,8192]{1,0:T(8,128)(2,1)S(1)}, bf16[128,8192]{1,0:T(8,128)(2,1)}, u32[]{:S(2)}) copy-start(bf16[128,8192]{1,0:T(8,128)(2,1)} %shard_map.128) | copy-start | bytes 6291460

commit v2 on v1

--- a/solution.py
+++ b/solution.py
@@ -288,6 +288,237 @@
     )(partial, gate)
 
 
+def experts_kernel(
+    n, ne, cap, hid_ref, pick_ref, pack_ref, unpack_ref, gain_ref, router_ref, wg_ref, wu_ref, wd_ref, o_ref,
+    wg, wu, wd, r_buf, rows, gains, normed, mine, p_buf, x_buf, s_buf, z_buf, w_buf,
+    w_sem, e_send, e_recv, n_send, n_recv, s_send, s_recv, x_send, x_recv, z_send, z_recv,
+    t_send, t_recv, own,
+):
+    me = lax.axis_index("seq")
+    place = lax.axis_index("exp")
+    nz, z, x = n // 2, me // 2, lax.rem(me, 2)
+    loads = [
+        pltpu.make_async_copy(src, dst, w_sem.at[t])
+        for t, (src, dst) in enumerate(((wg_ref, wg), (wu_ref, wu), (wd_ref, wd)))
+    ]
+    for copy in loads:
+        copy.start()
+    pos = (1 - x) * z + x * (n - 1 - z)
+    ways = (1, n - 1)
+    nexts = [{"seq": ring_device(lax.rem(pos + way, n), n)} for way in ways]
+    partner = {"seq": z * 2 + 1 - x}
+    along = [{"seq": lax.rem(z + k, nz) * 2 + x} for k in range(1, nz)]
+    others = [{"exp": lax.rem(place + i, ne)} for i in range(1, ne)]
+    flat_at = me * ne + place
+    everyone = n * ne
+
+    barrier = pltpu.get_barrier_semaphore()
+
+    def hello(i, carry):
+        at = lax.rem(flat_at + i, everyone)
+        pl.semaphore_signal(
+            barrier, inc=1, device_id={"seq": at // ne, "exp": lax.rem(at, ne)}, device_id_type=MESH
+        )
+        return carry
+
+    lax.fori_loop(1, everyone, hello, 0)
+    r_buf[...] = jnp.dot(pick_ref[...], hid_ref[...], preferred_element_type=jnp.float32).astype(jnp.bfloat16)
+    width = r_buf.shape[1]
+    pl.semaphore_wait(barrier, everyone - 1)
+
+    def piece(seq_at, exp_at):
+        return rows.at[cut(seq_at * cap, cap), cut(exp_at * width, width)]
+
+    def kind(e):
+        return (2 * e) // ne
+
+    local = pltpu.make_async_copy(r_buf.at[cut(place * cap, cap), :], piece(me, place), own.at[0])
+    local.start()
+    own_gain = pltpu.make_async_copy(
+        gain_ref.at[pl.ds(kind(place), 1), :], gains.at[:, cut(place * width, width)], own.at[1]
+    )
+    own_gain.start()
+    first = []
+    scales = []
+    for i in range(1, ne):
+        to = lax.rem(place + i, ne)
+        first.append(
+            push(r_buf.at[cut(to * cap, cap), :], piece(me, place), e_send.at[i], e_recv.at[i], others[i - 1])
+        )
+    hops = {}
+    for t in range(n // 2):
+        for i in range(ne):
+            if t == 0:
+                local.wait() if i == 0 else first[i - 1].wait_recv()
+            for d in range(2):
+                if t:
+                    hops[i, d, t - 1].wait_recv()
+                if t == n // 2 - 1 and i % 2 != d:
+                    continue
+                seq_at = ring_device(lax.rem(pos + n + t * (ways[1 - d]), n), n)
+                part = piece(seq_at, lax.rem(place + ne - i, ne))
+                at = (i * 2 + d) * (n // 2) + t
+                hops[i, d, t] = push(part, part, s_send.at[at], s_recv.at[at], nexts[d])
+        if t == 0:
+            for i in range(1, ne):
+                to = lax.rem(place + i, ne)
+                scales.append(
+                    push(
+                        gain_ref.at[pl.ds(kind(to), 1), :], gains.at[:, cut(place * width, width)],
+                        n_send.at[i], n_recv.at[i], others[i - 1],
+                    )
+                )
+    own_gain.wait()
+    for copy in scales:
+        copy.wait_recv()
+    for i in range(ne):
+        hops[i, i % 2, n // 2 - 1].wait_recv()
+
+    count = pack_ref.shape[0]
+    depth = ne * width
+    square = jnp.zeros((count, 1), jnp.float32)
+    for e in range(ne):
+        span = slice(e * width, (e + 1) * width)
+        packed = jnp.dot(pack_ref[...], rows[:, span], preferred_element_type=jnp.float32)
+        square += jnp.sum(packed * packed, axis=1, keepdims=True)
+        normed[:, span] = packed.astype(jnp.bfloat16)
+    inverse = lax.rsqrt(square / depth + 1e-05)
+    logits = jnp.zeros((count, 1), jnp.float32)
+    for e in range(ne):
+        span = slice(e * width, (e + 1) * width)
+        scaled = (normed[:, span].astype(jnp.float32) * inverse * gains[:, span]).astype(jnp.bfloat16)
+        normed[:, span] = scaled
+        logits += jnp.sum(scaled.astype(jnp.float32) * router_ref[:, span], axis=1, keepdims=True)
+    gate = jax.nn.sigmoid(logits)
+
+    loads[0].wait()
+    loads[1].wait()
+    hidden = wg.shape[1]
+    block = depth // n
+
+    def expand(j, sums):
+        at = cut(j * block, block)
+        part = normed[:, at]
+        return (
+            sums[0] + jnp.dot(part, wg[at, :], preferred_element_type=jnp.float32),
+            sums[1] + jnp.dot(part, wu[at, :], preferred_element_type=jnp.float32),
+        )
+
+    zero = jnp.zeros((count, hidden), jnp.float32)
+    gate_part, up_part = lax.fori_loop(0, n, expand, (zero, zero))
+    inner = (jax.nn.silu(gate_part) * up_part).astype(jnp.bfloat16)
+    loads[2].wait()
+
+    def partial(k, side):
+        at = lax.rem(z + k, nz) * 2 + side
+        return jnp.dot(inner, wd[:, cut(at * block, block)], preferred_element_type=jnp.float32)
+
+    order = list(range(1, nz)) + [0]
+    pairs = {}
+    for k in order:
+        p_buf[k] = partial(k, 1 - x).astype(jnp.bfloat16)
+        pairs[k] = push(p_buf.at[k], x_buf.at[k], x_send.at[k], x_recv.at[k], partner)
+    for k in order:
+        mine[k] = partial(k, x)
+    sent = []
+    for k in order:
+        pairs[k].wait_recv()
+        if k:
+            s_buf[k] = (mine[k] + x_buf[k].astype(jnp.float32)).astype(jnp.bfloat16)
+            sent.append(push(s_buf.at[k], z_buf.at[k], z_send.at[k], z_recv.at[k], along[k - 1]))
+    total = mine[0] + x_buf[0].astype(jnp.float32)
+    for k in range(1, nz):
+        sent[k - 1].wait_recv()
+        total += z_buf[k].astype(jnp.float32)
+    weighted = (gate * total).astype(jnp.bfloat16)
+    w_buf[...] = jnp.dot(unpack_ref[...], weighted, preferred_element_type=jnp.float32).astype(jnp.bfloat16)
+
+    per = n // ne
+    target = me // per
+    turn = lax.rem(me, per)
+
+    def deliver(i):
+        to = lax.rem(me + i, n)
+        at = turn * ne + place
+        return pltpu.make_async_remote_copy(
+            src_ref=w_buf.at[cut(to * cap, cap), :],
+            dst_ref=o_ref.at[cut(place * cap, cap), cut(turn * block, block)],
+            send_sem=t_send.at[i], recv_sem=t_recv.at[at],
+            device_id={"seq": to, "exp": target}, device_id_type=MESH,
+        )
+
+    home = pltpu.make_async_copy(
+        w_buf.at[cut(me * cap, cap), :], o_ref.at[cut(place * cap, cap), cut(turn * block, block)], own.at[2]
+    )
+    stays = target == place
+    for i in range(1, n):
+        deliver(i).start()
+
+    @pl.when(stays)
+    def _():
+        home.start()
+
+    @pl.when(jnp.logical_not(stays))
+    def _():
+        deliver(0).start()
+
+    for k in range(per):
+        for e in range(ne):
+            arrival = pltpu.make_async_remote_copy(
+                src_ref=w_buf.at[cut(me * cap, cap), :],
+                dst_ref=o_ref.at[e * cap : (e + 1) * cap, k * block : (k + 1) * block],
+                send_sem=t_send.at[0], recv_sem=t_recv.at[k * ne + e],
+                device_id=partner, device_id_type=MESH,
+            )
+
+            @pl.when(jnp.logical_not(stays & (turn == k) & (place == e)))
+            def _():
+                arrival.wait_recv()
+
+    @pl.when(stays)
+    def _():
+        home.wait()
+
+    @pl.when(jnp.logical_not(stays))
+    def _():
+        deliver(0).wait_send()
+
+    for i in range(1, n):
+        deliver(i).wait_send()
+    for copy in first + scales + list(hops.values()) + list(pairs.values()) + sent:
+        copy.wait_send()
+
+
+def run_experts(hidden_state, pick_rows, pack, unpack, norm_gain, router_row, w_gate, w_up, w_down, n, ne):
+    count, slots = pack.shape
+    cap = slots // n
+    width = hidden_state.shape[1]
+    depth, hidden = w_gate.shape
+    nz, block = n // 2, depth // n
+    bf, f32 = jnp.bfloat16, jnp.float32
+    inside = pl.BlockSpec(memory_space=pltpu.VMEM)
+    anywhere = pl.BlockSpec(memory_space=pl.ANY)
+    slab = pltpu.VMEM((nz, count, block), bf)
+    sems = lambda size: pltpu.SemaphoreType.DMA((size,))
+    return pl.pallas_call(
+        functools.partial(experts_kernel, n, ne, cap),
+        out_shape=jax.ShapeDtypeStruct((ne * cap, width), bf),
+        in_specs=[inside] * 6 + [anywhere] * 3,
+        out_specs=anywhere,
+        scratch_shapes=[
+            pltpu.VMEM((depth, hidden), bf), pltpu.VMEM((depth, hidden), bf), pltpu.VMEM((hidden, depth), bf),
+            pltpu.VMEM((ne * cap, width), bf), pltpu.VMEM((slots, depth), bf), pltpu.VMEM((1, depth), f32),
+            pltpu.VMEM((count, depth), bf), pltpu.VMEM((nz, count, block), f32),
+            slab, slab, slab, slab, pltpu.VMEM((slots, block), bf),
+            sems(3), sems(ne), sems(ne), sems(ne), sems(ne), sems(ne * n), sems(ne * n),
+            sems(nz), sems(nz), sems(nz), sems(nz), sems(n), sems(n), sems(3),
+        ],
+        compiler_params=pltpu.CompilerParams(
+            collective_id=2, has_side_effects=True, vmem_limit_bytes=56 * 1024 * 1024
+        ),
+    )(hidden_state, pick_rows, pack, unpack, norm_gain, router_row, w_gate, w_up, w_down)
+
+
 def flash_kernel(block, border_ref, q_ref, k_ref, v_ref, o_ref):
     at = pl.program_id(1)
     border = border_ref[0]
@@ -828,10 +1059,6 @@
     )
     hidden_state = (residual.astype(jnp.float32) + mixed).astype(jnp.bfloat16)
     hidden_wide = hidden_state.astype(jnp.float32)
-    square_total = lax.psum(jnp.sum(hidden_wide * hidden_wide, axis=1), "exp")
-    inverse = lax.rsqrt(square_total / D + 1e-05)
-    gain_rows = jnp.where(modality[:, None] == 0, norm_gain[0][None, :], norm_gain[1][None, :])
-    normed = (hidden_wide * inverse[:, None] * gain_rows).astype(jnp.bfloat16)
     capacity = tokens // 32
     inside = (picks >= start_row) & (picks < start_row + tokens)
     slot_index = jnp.cumsum(inside.astype(jnp.int32), axis=1) - 1
@@ -840,20 +1067,21 @@
     )
     local_index = jnp.sum(jnp.where(matched, picks[:, None, :] - start_row, 0), axis=2)
     filled = jnp.any(matched, axis=2)
-    rows_out = jnp.take(normed, local_index.reshape(-1), axis=0)
-    rows_out = jnp.where(filled.reshape(-1, 1), rows_out, jnp.zeros_like(rows_out))
-    piece = share_rows(rows_out, n_seq, n_exp)
-    expert_rows = lax.dynamic_slice_in_dim(piece, seq_pos * capacity, capacity, 0)
-    logits = jnp.dot(expert_rows, router, preferred_element_type=jnp.float32)[:, 0]
-    gate_part = jnp.dot(piece, w_gate[0], preferred_element_type=jnp.float32)
-    up_part = jnp.dot(piece, w_up[0], preferred_element_type=jnp.float32)
-    inner_act = (jax.nn.silu(gate_part) * up_part).astype(jnp.bfloat16)
-    partial = jnp.dot(inner_act, w_down[0], preferred_element_type=jnp.float32).astype(jnp.bfloat16)
-    returned = sum_rows(partial, jax.nn.sigmoid(logits)[:, None], n_seq, n_exp)
     placing = (
         (jnp.arange(tokens, dtype=jnp.int32)[:, None] == local_index.reshape(1, -1))
         & filled.reshape(1, -1)
     ).astype(jnp.bfloat16)
+    picked = lax.dynamic_index_in_dim(picks, lax.axis_index("exp"), 0, keepdims=False)
+    home = picked // tokens
+    rank = jnp.arange(picked.shape[0], dtype=jnp.int32) - jnp.sum(
+        (home[None, :] < home[:, None]).astype(jnp.int32), axis=1
+    )
+    slot = home * capacity + rank
+    pack = (slot[:, None] == jnp.arange(n_seq * capacity, dtype=jnp.int32)[None, :]).astype(jnp.bfloat16)
+    returned = run_experts(
+        hidden_state, placing.T, pack, pack.T, norm_gain, router.astype(jnp.float32).reshape(1, -1),
+        w_gate[0], w_up[0], w_down[0], n_seq, n_exp,
+    )
     expert_add = jnp.dot(placing, returned, preferred_element_type=jnp.float32)
     return (hidden_wide + expert_add).astype(jnp.bfloat16)
 

time: 206 us -> 170 us (0.83); the launches traced: 202 us -> 169 us
  matrix products: 32.8 us -> 17.5 us
  Pallas kernels: 150 us -> 143 us
  blocking collectives: 5.35 us -> 0 us
  local copies, waits for them, and re-layouts: 7.53 us -> 3.87 us
    dot_general x3 -> x0, matrix products: 15.2 us -> none  [the longest x1 9.6 us: shards(): jnp.dot(inner_act, w_down[0], preferred_element_type=jnp.float32)]
    pallas_call x2 -> x1, Pallas kernels: 70 us -> 62.7 us  [run_experts(): pl.pallas_call(functools.partial(experts_kernel, n, ne, cap), out_shape=j...]
    psum x1 -> x0, blocking collectives: 5.35 us -> none  [shards(): square_total = lax.psum(jnp.sum(hidden_wide * hidden_wide, axis=1), 'exp')]
    gather x1 -> x0, local copies, waits for them, and re-layouts: 2.85 us -> none  [shards(): rows_out = jnp.take(normed, local_index.reshape(-1), axis=0)]
where the time goes in v2:
time: 170 us; the launch traced here: 169 us
  Pallas kernels  143 us (84%)
  matrix products  17.5 us (10%)
  other arithmetic  4.79 us (3%)
  local copies, waits for them, and re-layouts  3.87 us (2%)
    pallas_call x1, Pallas kernels, attend_by_chain(): pl.pallas_call(functools.partial(chain_kernel, nz, n_exp, group, None), o...  80 us
    pallas_call x1, Pallas kernels, run_experts(): pl.pallas_call(functools.partial(experts_kernel, n, ne, cap), out_shape=j...  62.7 us
    dot_general x1, matrix products, shards(): mixed = jnp.dot(attended, out_proj, preferred_element_type=jnp.float32)  14.6 us
    unnamed x14, local copies, waits for them, and re-layouts  3.69 us

profile of v2, /device:TPU:5, one launch (start us, length us, event | category | flops | bytes accessed | tf_op | source)
XLA Modules:
  0.0 169.0 jit_solution(2027279847319959394)
XLA Ops:
  0.0 1.4 convert_reduce_fusion.1
  1.4 0.0 copy-start
  1.4 1.2 copy-done
  2.6 0.0 copy-start.1
  2.6 1.2 copy-done.1
  3.8 0.0 copy-start.2
  3.8 1.2 copy-done.2
  5.0 0.0 copy-start.6
  5.0 80.0 %shard_map.118 = bf16[512,4096]{1,0:T(8,128)(2,1)} custom-call(s32[1]{0:T(128)} %bitcast.border_ref, bf16[512,1024]{1,0:T(8,128)(2,1)S(1)} %copy-done, bf16[512,1024]{1,0:T(8,128)(2,1)S(1)} %copy-done.1, bf16[512,1024]{1,0:T(8,128)(2,1)S(1)} %copy-done.2), custom_call_target="tpu_custom_call" | custom-call | tf_op jit(solution)/shard_map/pallas_call | solution.py:938
  85.1 0.0 copy-done.6
  85.1 0.0 copy-start.5
  85.1 0.0 copy-start.4
  85.1 14.6 %add_convert_fusion.1.hid_ref = bf16[512,2048]{1,0:T(8,128)(2,1)} fusion(bf16[512,2048]{1,0:T(8,128)(2,1)S(1)} %copy-done.6, bf16[512,4096]{1,0:T(8,128)(2,1)} %shard_map.118, bf16[4096,2048]{1,0:T(8,128)(2,1)} %param.18), kind=kOutput, calls=%fused_computation.1 | convolution fusion | flops 8593080320 | bytes 25165824 | tf_op jit(solution)/shard_map/dot_general | solution.py:1055
  99.7 0.0 copy-done.5
  99.7 0.2 reduce_window_sum.11
  99.9 0.1 select_reduce_fusion
  100.1 0.1 eq.67
  100.2 0.2 fusion.8
  100.3 0.1 and.54
  100.4 0.7 fusion.4.pick_ref
  101.2 0.2 convert_reduce_fusion
  101.4 0.7 fusion.9.pack_ref
  102.1 0.6 fusion.6.unpack_ref
  102.7 0.0 copy-done.4
  102.7 0.6 bitcast_convert_fusion.router_ref
  103.3 0.0 copy-start.3
  103.3 62.7 %shard_map.119 = bf16[64,2048]{1,0:T(8,128)(2,1)} custom-call(bf16[512,2048]{1,0:T(8,128)(2,1)} %add_convert_fusion.1.hid_ref, bf16[64,512]{1,0:T(8,128)(2,1)} %fusion.4.pick_ref, bf16[64,128]{1,0:T(8,128)(2,1)} %fusion.9.pack_ref, bf16[128,64]{1,0:T(8,128)(2,1)} %fusion.6.unpack_ref, f32[2,2048]{1,0:T(2,128)} %gain_ref.1, ...), custom_call_target="tpu_custom_call" | custom-call | tf_op jit(solution)/shard_map/pallas_call | solution.py:503
  166.0 0.0 copy-done.3
  166.0 3.0 %add_convert_fusion = bf16[512,2048]{1,0:T(8,128)(2,1)} fusion(bf16[512,2048]{1,0:T(8,128)(2,1)S(1)} %copy-done.3, bf16[64,2048]{1,0:T(8,128)(2,1)} %shard_map.119, s32[64]{0:T(128)S(1)} %eq.67, pred[64]{0:T(512)(128)(4,1)S(1)} %and.54), kind=kOutput, calls=%fused_computation | convolution fusion | flops 137428992 | bytes 4456768 | tf_op jit(solution)/shard_map/dot_general | solution.py:1085
  (5 shorter events, 0.1 us)
Async XLA Ops:
  1.4 1.2 copy-start
  2.6 1.2 copy-start.1
  3.8 1.2 copy-start.2
  5.0 80.1 %copy-start.6 = (bf16[512,2048]{1,0:T(8,128)(2,1)S(1)}, bf16[512,2048]{1,0:T(8,128)(2,1)}, u32[]{:S(2)}) copy-start(bf16[512,2048]{1,0:T(8,128)(2,1)} %param.13) | copy-start | bytes 6291460
  85.1 14.6 %copy-start.5 = (s32[4,64]{1,0:T(4,128)S(1)}, s32[4,64]{1,0:T(4,128)}, u32[]{:S(2)}) copy-start(s32[4,64]{1,0:T(4,128)} %param.20) | copy-start | bytes 3076
  85.1 17.6 %copy-start.4 = (bf16[8192,1]{0,1:T(2,128)(2,1)S(1)}, bf16[8192,1]{0,1:T(2,128)(2,1)}, u32[]{:S(2)}) copy-start(bf16[8192,1]{0,1:T(2,128)(2,1)} %param.21) | copy-start | bytes 49156
  103.3 62.7 %copy-start.3 = (bf16[512,2048]{1,0:T(8,128)(2,1)S(1)}, bf16[512,2048]{1,0:T(8,128)(2,1)}, u32[]{:S(2)}) copy-start(bf16[512,2048]{1,0:T(8,128)(2,1)} %add_convert_fusion.1.hid_ref) | copy-start | bytes 6291460

commit v3 on v2

--- a/solution.py
+++ b/solution.py
@@ -591,11 +591,11 @@
 
 
 def chain_kernel(
-    nz, ne, group, causal_span, border_ref, q_ref, k_ref, v_ref, o_ref,
-    q0, q1, q2, kb, vb, o0, o1, c0, c1, s2, s1, p2, p1, ls2, ls1, lp2, lp1, fin, back,
+    nz, ne, group, docs_ref, q_ref, k_ref, v_ref, res_ref, w_ref, o_ref,
+    q0, q1, q2, kb, vb, o0, o1, c0, c1, s2, s1, p2, p1, ls2, ls1, lp2, lp1, back, att, proj, acc, res,
     load, x_send, x_recv, d0_send, d0_recv, d1_send, d1_recv, u2_send, u2_recv, g2_send, g2_recv,
     u1_send, u1_recv, g1_send, g1_recv, b_send, b_recv, y_send, y_recv, m_send, m_recv,
-    r_send, r_recv, own,
+    r_send, r_recv, w_sem, res_sem,
 ):
     me = lax.axis_index("seq")
     place = lax.axis_index("exp")
@@ -611,7 +611,9 @@
     far_place = lax.rem(y + 1, ny) * 2 + core
     far = {"exp": far_place}
     has1, has2, low1 = z + 1 < nz, z + 2 < nz, z >= 1
-    border = border_ref[0]
+    border = jnp.sum(
+        jnp.sum((docs_ref[...] == 0).astype(jnp.int32), axis=1, keepdims=True), axis=0, keepdims=True
+    )
     scale = math.log2(math.e) / math.sqrt(HD)
     greet([up, down, partner, sibling, far])
 
@@ -660,25 +662,33 @@
             remote(ls1.at[t], lp1.at[t], g1_send.at[t], g1_recv.at[t], up),
         )
 
+    def spot(at, t):
+        return att.at[t, :, cut(at * HD, HD)]
+
     def give_back(t):
-        return remote(back.at[t // 2], fin.at[t], b_send.at[t // 2], b_recv.at[t // 2], partner)
-
-    def spot(at, t):
-        j = lax.rem(t, 2)
-        side = x + j * (1 - 2 * x)
-        return o_ref.at[:, cut(((at * 2 + side) * group + t // 2) * HD, HD)]
-
-    def keep(t):
-        return pltpu.make_async_copy(fin.at[t], spot(place, t), own.at[t])
+        return remote(back.at[t // 2], spot(place, t), b_send.at[t // 2], b_recv.at[t // 2], partner)
 
     def to_far(t):
-        return remote(fin.at[t], spot(place, t), y_send.at[t], y_recv.at[t], far)
+        return remote(spot(place, t), spot(place, t), y_send.at[t], y_recv.at[t], far)
 
     def to_sibling(t):
-        return remote(fin.at[t], spot(place, t), m_send.at[t], m_recv.at[t], sibling)
+        return remote(spot(place, t), spot(place, t), m_send.at[t], m_recv.at[t], sibling)
 
     def relay(t):
         return remote(spot(far_place, t), spot(far_place, t), r_send.at[t], r_recv.at[t], sibling)
+
+    def proj_loads(t):
+        side = x + (t % 2) * (1 - 2 * x)
+        return [
+            pltpu.make_async_copy(
+                w_ref.at[cut(((e * 2 + side) * group + t // 2) * HD, HD), :],
+                proj.at[t, e * HD : (e + 1) * HD, :],
+                w_sem.at[t, e],
+            )
+            for e in range(ne)
+        ]
+
+    res_load = pltpu.make_async_copy(res_ref, res, res_sem)
 
     tile = HD
     tiles = tokens // tile
@@ -688,29 +698,46 @@
         jnp.int32, (tile, tile), 1
     )
 
-    def attend(q_of, h, level, t, put):
-        j = lax.rem(t, 2)
-        side = x + j * (1 - 2 * x)
+    big = 2 * tile
+    at = lax.broadcasted_iota(jnp.int32, (big, tokens), 1)
+
+    def attend(q_of, level, t, put, blocks):
+        h = t // 2
+        side = x + lax.rem(t, 2) * (1 - 2 * x)
         base = ((z + level) * 2 + side) * tokens - key_base
         edge = border - key_base
-        keys, vals = kb[h], vb[h]
-        at = lax.broadcasted_iota(jnp.int32, (tile, span), 1)
-        for r in range(tiles):
-            rows = base + r * tile + lax.broadcasted_iota(jnp.int32, (tile, 1), 0)
+
+        def score(r):
+            rows = base + r * big + lax.broadcasted_iota(jnp.int32, (big, 1), 0)
             low = jnp.where(rows >= edge, edge, -key_base)
-            s = lax.dot_general(
-                q_of[r * tile : (r + 1) * tile, :], keys, (((1,), (1,)), ((), ())),
-                preferred_element_type=jnp.float32,
-            )
-            seen = at >= low
-            if level == 0:
-                seen = seen & (at <= rows)
-            s = jnp.where(seen, s, -1e30)
-            top = jnp.max(s, axis=1, keepdims=True) * scale
-            p = jnp.exp2(s * scale - top)
-            total = jnp.sum(p, axis=1, keepdims=True)
-            out = jnp.dot(p.astype(jnp.bfloat16), vals, preferred_element_type=jnp.float32)
-            put(r, out / total, top + jnp.log2(total))
+            out = []
+            for b in range(blocks):
+                s = lax.dot_general(
+                    q_of[r * big : (r + 1) * big, :], kb[h, b * tokens : (b + 1) * tokens, :],
+                    (((1,), (1,)), ((), ())), preferred_element_type=jnp.float32,
+                )
+                seen = at >= low - b * tokens
+                if level == 0 and b == blocks - 1:
+                    seen = seen & (at <= rows - b * tokens)
+                out.append(jnp.where(seen, s, -1e30))
+            return out
+
+        later = score(0)
+        for r in range(tokens // big):
+            now = later
+            if (r + 1) * big < tokens:
+                later = score(r + 1)
+            top = jnp.max(functools.reduce(jnp.maximum, now), axis=1, keepdims=True) * scale
+            total = jnp.zeros((big, 1), jnp.float32)
+            out = jnp.zeros((big, HD), jnp.float32)
+            for b, s in enumerate(now):
+                p = jnp.exp2(s * scale - top)
+                total += jnp.sum(p, axis=1, keepdims=True)
+                out += jnp.dot(
+                    p.astype(jnp.bfloat16), vb[h, b * tokens : (b + 1) * tokens, :],
+                    preferred_element_type=jnp.float32,
+                )
+            put(r * big, out / total, top + jnp.log2(total))
 
     def flat(level):
         return jnp.sum(jnp.where(diagonal, level, 0.0), axis=0, keepdims=True)
@@ -732,6 +759,11 @@
         for copy in loads(h):
             copy.start()
 
+    for t in range(steps):
+        for copy in proj_loads(t):
+            copy.start()
+    res_load.start()
+
     def send_own(t):
         @pl.when(lax.rem(t, 2) == 0)
         def _():
@@ -755,7 +787,6 @@
                 q_further(t).start()
 
     def spread(t):
-        keep(t).start()
         to_far(t).start()
         to_sibling(t).start()
 
@@ -785,13 +816,20 @@
         def _():
             q_further(i).wait_recv()
 
-            def put(r, out, level):
-                s2[i, r * tile : (r + 1) * tile, :] = out.astype(jnp.bfloat16)
-                ls2[i, r : r + 1, :] = flat(level)
-
-            attend(q2.at[i], i // 2, 2, i, put)
+            def put(at, out, level):
+                s2[i, at : at + big, :] = out.astype(jnp.bfloat16)
+                for r in range(big // tile):
+                    row = at // tile + r
+                    ls2[i, row : row + 1, :] = flat(level[r * tile : (r + 1) * tile])
+
+            attend(q2.at[i], 2, i, put, 2)
             for copy in part2_up(i):
                 copy.start()
+
+        @pl.when(i == 1)
+        def _():
+            res_load.wait()
+            acc[...] = res[...].astype(jnp.float32)
 
         t1 = i - 1
 
@@ -818,11 +856,11 @@
 
         @pl.when(live & has1)
         def _():
-            def put(r, out, level):
-                o1[i, r * tile : (r + 1) * tile, :] = out
-                c1[i, r * tile : (r + 1) * tile, :] = level
-
-            attend(q1.at[i], i // 2, 1, i, put)
+            def put(at, out, level):
+                o1[i, at : at + big, :] = out
+                c1[i, at : at + big, :] = level
+
+            attend(q1.at[i], 1, i, put, 2)
 
         t0 = i - 2
 
@@ -845,7 +883,7 @@
             @pl.when(lax.rem(t0, 2) == 0)
             def _():
                 def put(r, out):
-                    fin[t0, r * tile : (r + 1) * tile, :] = out.astype(jnp.bfloat16)
+                    att[t0, r * tile : (r + 1) * tile, cut(place * HD, HD)] = out.astype(jnp.bfloat16)
 
                 finish(put)
                 spread(t0)
@@ -860,11 +898,19 @@
 
         @pl.when(live)
         def _():
-            def put(r, out, level):
-                o0[i, r * tile : (r + 1) * tile, :] = out
-                c0[i, r * tile : (r + 1) * tile, :] = level
-
-            attend(q0.at[i], i // 2, 0, i, put)
+            def put(at, out, level):
+                o0[i, at : at + big, :] = out
+                c0[i, at : at + big, :] = level
+
+            first_half = lax.rem(i, 2) == x
+
+            @pl.when(first_half)
+            def _():
+                attend(q0.at[i], 0, i, put, 1)
+
+            @pl.when(jnp.logical_not(first_half))
+            def _():
+                attend(q0.at[i], 0, i, put, 2)
 
         t4 = i - 3
 
@@ -880,14 +926,24 @@
             to_far(t5).wait_recv()
             relay(t5).start()
 
+        t6 = i - 6
+
+        @pl.when((t6 >= 0) & (t6 < steps))
+        def _():
+            to_sibling(t6).wait_recv()
+            relay(t6).wait_recv()
+            for copy in proj_loads(t6):
+                copy.wait()
+
+            acc[...] += jnp.dot(att[t6], proj[t6], preferred_element_type=jnp.float32)
+
         return carry
 
-    lax.fori_loop(0, steps + 5, step, 0)
+    lax.fori_loop(0, steps + 6, step, 0)
+    o_ref[...] = acc[...].astype(o_ref.dtype)
+
 
     def settle(t, carry):
-        to_sibling(t).wait_recv()
-        relay(t).wait_recv()
-        keep(t).wait()
         to_far(t).wait_send()
         to_sibling(t).wait_send()
         relay(t).wait_send()
@@ -921,13 +977,14 @@
     lax.fori_loop(0, steps, settle, 0)
 
 
-def attend_by_chain(queries, keys, values, documents, n, n_exp):
+def attend_by_chain(queries, keys, values, documents, residual, out_proj, n, n_exp):
     tokens, width = queries.shape
     group = width // HD // 2
     steps = 2 * group
     nz = n // 2
-    border = jnp.sum((documents == 0).astype(jnp.int32)).reshape(1)
-    anywhere = pl.BlockSpec(memory_space=pl.ANY)
+    features = out_proj.shape[1]
+    outside = pl.BlockSpec(memory_space=pltpu.HBM)
+    inside = pl.BlockSpec(memory_space=pltpu.VMEM)
     bf, f32 = jnp.bfloat16, jnp.float32
     chunks = pltpu.VMEM((steps, tokens, HD), bf)
     side = pltpu.VMEM((group, 2 * tokens, HD), bf)
@@ -936,17 +993,20 @@
     flats = pltpu.VMEM((steps, max(8, tokens // HD), HD), f32)
     sems = lambda count: pltpu.SemaphoreType.DMA((count,))
     return pl.pallas_call(
-        functools.partial(chain_kernel, nz, n_exp, group, None),
-        out_shape=jax.ShapeDtypeStruct((tokens, n_exp * width), queries.dtype),
-        in_specs=[pl.BlockSpec(memory_space=pltpu.SMEM)] + [anywhere] * 3,
-        out_specs=anywhere,
+        functools.partial(chain_kernel, nz, n_exp, group),
+        out_shape=jax.ShapeDtypeStruct((tokens, features), queries.dtype),
+        in_specs=[inside] + [outside] * 5,
+        out_specs=inside,
         scratch_shapes=[chunks] * 3 + [side] * 2 + [wide] * 2 + [thin] * 2 + [chunks] * 4 + [flats] * 4
-        + [chunks, pltpu.VMEM((group, tokens, HD), bf)]
-        + [sems(3 * group)] * 3 + [sems(steps)] * 12 + [sems(group)] * 2 + [sems(steps)] * 6 + [sems(steps)],
+        + [pltpu.VMEM((group, tokens, HD), bf), pltpu.VMEM((steps, tokens, n_exp * HD), bf)]
+        + [pltpu.VMEM((steps, n_exp * HD, features), bf), pltpu.VMEM((tokens, features), f32)]
+        + [pltpu.VMEM((tokens, features), bf)]
+        + [sems(3 * group)] * 3 + [sems(steps)] * 12 + [sems(group)] * 2 + [sems(steps)] * 6
+        + [pltpu.SemaphoreType.DMA((steps, n_exp)), pltpu.SemaphoreType.DMA(())],
         compiler_params=pltpu.CompilerParams(
-            collective_id=0, has_side_effects=True, vmem_limit_bytes=48 * 1024 * 1024
+            collective_id=0, has_side_effects=True, vmem_limit_bytes=60 * 1024 * 1024
         ),
-    )(border, queries, keys, values)
+    )(documents.reshape(-1, HD), queries, keys, values, residual, out_proj)
 
 
 def attend_by_token(queries, keys, values, documents):
@@ -1048,16 +1108,14 @@
     seq_pos = lax.axis_index("seq")
     start_row = seq_pos * tokens
     n_seq, n_exp = lax.axis_size("seq"), lax.axis_size("exp")
-    if (queries.shape[1] // HD) % n_seq == 0 and n_exp % 2 == 0:
-        attended = attend_by_chain(queries, keys, values, documents, n_seq, n_exp)
+    if (queries.shape[1] // HD) % n_seq == 0 and n_exp == 4:
+        hidden_state = attend_by_chain(
+            queries, keys, values, documents, residual, out_proj, n_seq, n_exp
+        )
     else:
         attended = attend_by_token(queries, keys, values, documents)
-    mixed = jnp.dot(
-        attended,
-        out_proj,
-        preferred_element_type=jnp.float32,
-    )
-    hidden_state = (residual.astype(jnp.float32) + mixed).astype(jnp.bfloat16)
+        mixed = jnp.dot(attended, out_proj, preferred_element_type=jnp.float32)
+        hidden_state = (residual.astype(jnp.float32) + mixed).astype(jnp.bfloat16)
     hidden_wide = hidden_state.astype(jnp.float32)
     capacity = tokens // 32
     inside = (picks >= start_row) & (picks < start_row + tokens)

time: 170 us -> 155 us (0.912)
  matrix products: 17.5 us -> 2.97 us
  local copies, waits for them, and re-layouts: 3.87 us -> 0.17 us
  other arithmetic: 4.79 us -> 7.6 us
    dot_general x1 -> x0, matrix products: 14.6 us -> none  [shards(): mixed = jnp.dot(attended, out_proj, preferred_element_type=jnp.float32)]
    unnamed x14 -> x2, local copies, waits for them, and re-layouts: 3.69 us -> 0.01 us
    pallas_call x1, Pallas kernels: 62.7 us -> 65.5 us  [run_experts(): pl.pallas_call(functools.partial(experts_kernel, n, ne, cap), out_shape=j...]
    pallas_call x1, Pallas kernels: 80 us -> 78 us  [attend_by_chain(): pl.pallas_call(functools.partial(chain_kernel, nz, n_exp, group), out_sha...]
where the time goes in v3:
time: 155 us; the launch traced here: 154 us
  Pallas kernels  144 us (93%)
  other arithmetic  7.6 us (5%)
  matrix products  2.97 us (2%)
    pallas_call x1, Pallas kernels, attend_by_chain(): pl.pallas_call(functools.partial(chain_kernel, nz, n_exp, group), out_sha...  78 us
    pallas_call x1, Pallas kernels, run_experts(): pl.pallas_call(functools.partial(experts_kernel, n, ne, cap), out_shape=j...  65.5 us

profile of v3, /device:TPU:5, one launch (start us, length us, event | category | flops | bytes accessed | tf_op | source)
XLA Modules:
  0.0 154.3 jit_solution(5995405868003049244)
XLA Ops:
  0.0 0.7 fusion.10
  0.7 0.7 and_select_fusion.1
  1.4 0.2 convert_reduce_fusion
  1.6 0.7 subtract_add_fusion
  2.3 0.7 fusion.11
  3.0 0.2 reduce_window_sum.11
  3.2 0.7 broadcast_add_fusion
  3.9 0.1 select_reduce_fusion
  4.0 0.2 fusion.8
  4.2 0.1 eq.59
  4.3 0.1 and.54
  4.4 0.7 fusion.9.pack_ref
  5.0 0.6 fusion.6.unpack_ref
  5.7 1.4 bitcast_convert_fusion.router_ref
  7.1 0.7 fusion.4.pick_ref
  7.8 78.0 %shard_map.118.hid_ref = bf16[512,2048]{1,0:T(8,128)(2,1)} custom-call(s32[32,128]{1,0:T(8,128)} %bitcast.23, bf16[512,1024]{1,0:T(8,128)(2,1)} %q_ref.1, bf16[512,1024]{1,0:T(8,128)(2,1)} %k_ref.1, bf16[512,1024]{1,0:T(8,128)(2,1)} %v_ref.1, bf16[512,2048]{1,0:T(8,128)(2,1)} %res_ref.1, bf16[4096,2048]{1,0:T(8,128)(2,1)} %w_ref.1), custom_call_target="tpu_custom_call" | custom-call | tf_op jit(solution)/shard_map/pallas_call | solution.py:995
  85.8 0.0 copy-start
  85.8 65.5 %shard_map.119 = bf16[64,2048]{1,0:T(8,128)(2,1)} custom-call(bf16[512,2048]{1,0:T(8,128)(2,1)} %shard_map.118.hid_ref, bf16[64,512]{1,0:T(8,128)(2,1)} %fusion.4.pick_ref, bf16[64,128]{1,0:T(8,128)(2,1)} %fusion.9.pack_ref, bf16[128,64]{1,0:T(8,128)(2,1)} %fusion.6.unpack_ref, f32[2,2048]{1,0:T(2,128)} %gain_ref.1, ...), custom_call_target="tpu_custom_call" | custom-call | tf_op jit(solution)/shard_map/pallas_call | solution.py:503
  151.3 0.0 copy-done
  151.3 3.0 %add_convert_fusion = bf16[512,2048]{1,0:T(8,128)(2,1)} fusion(bf16[512,2048]{1,0:T(8,128)(2,1)S(1)} %copy-done, bf16[64,2048]{1,0:T(8,128)(2,1)} %shard_map.119, s32[64]{0:T(128)S(1)} %eq.59, pred[64]{0:T(512)(128)(4,1)S(1)} %and.54), kind=kOutput, calls=%fused_computation | convolution fusion | flops 137428992 | bytes 4456768 | tf_op jit(solution)/shard_map/dot_general | solution.py:1143
Async XLA Ops:
  85.8 65.5 %copy-start = (bf16[512,2048]{1,0:T(8,128)(2,1)S(1)}, bf16[512,2048]{1,0:T(8,128)(2,1)}, u32[]{:S(2)}) copy-start(bf16[512,2048]{1,0:T(8,128)(2,1)} %shard_map.118.hid_ref) | copy-start | bytes 6291460

commit v4 on v3

--- a/solution.py
+++ b/solution.py
@@ -289,8 +289,8 @@
 
 
 def experts_kernel(
-    n, ne, cap, hid_ref, pick_ref, pack_ref, unpack_ref, gain_ref, router_ref, wg_ref, wu_ref, wd_ref, o_ref,
-    wg, wu, wd, r_buf, rows, gains, normed, mine, p_buf, x_buf, s_buf, z_buf, w_buf,
+    n, ne, cap, hid_ref, pick_ref, gain_ref, router_ref, wg_ref, wu_ref, wd_ref, o_ref, place_ref,
+    wg, wu, wd, r_buf, rows, gains, gate_sum, up_sum, mine, p_buf, x_buf, s_buf, z_buf, w_buf,
     w_sem, e_send, e_recv, n_send, n_recv, s_send, s_recv, x_send, x_recv, z_send, z_recv,
     t_send, t_recv, own,
 ):
@@ -322,7 +322,37 @@
         return carry
 
     lax.fori_loop(1, everyone, hello, 0)
-    r_buf[...] = jnp.dot(pick_ref[...], hid_ref[...], preferred_element_type=jnp.float32).astype(jnp.bfloat16)
+    tokens, count = hid_ref.shape[0], pick_ref.shape[1]
+
+    def counted(shape, axis):
+        return lax.broadcasted_iota(jnp.int32, shape, axis)
+
+    def upright(row):
+        same = counted((count, count), 0) == counted((count, count), 1)
+        return jnp.sum(jnp.where(same, row, 0), axis=1, keepdims=True)
+
+    def chosen(seen):
+        return jnp.where(seen, 1.0, 0.0).astype(jnp.bfloat16)
+
+    def crossed(a, b):
+        return lax.dot_general(a, b, (((0,), (0,)), ((), ())), preferred_element_type=jnp.float32)
+
+    for e in range(ne):
+        local_at = upright(pick_ref[e : e + 1, :]) - me * tokens
+        before = jnp.sum((local_at < 0).astype(jnp.int32), axis=0, keepdims=True)
+        turns = chosen(counted((count, cap), 0) - before == counted((count, cap), 1))
+        hits = chosen(local_at == counted((count, tokens), 1))
+        place_ref[e * cap : (e + 1) * cap, :] = crossed(turns, hits).astype(jnp.bfloat16)
+    whole_at = upright(pick_ref[pl.ds(place, 1), :])
+    slot = counted((1, n * cap), 1)
+    begin = (slot // cap) * tokens
+    before = jnp.sum((whole_at < begin).astype(jnp.int32), axis=0, keepdims=True)
+    pack = chosen(
+        (whole_at >= begin)
+        & (whole_at < begin + tokens)
+        & (counted((count, n * cap), 0) - before == lax.rem(slot, cap))
+    )
+    r_buf[...] = jnp.dot(place_ref[...], hid_ref[...], preferred_element_type=jnp.float32).astype(jnp.bfloat16)
     width = r_buf.shape[1]
     pl.semaphore_wait(barrier, everyone - 1)
 
@@ -345,68 +375,75 @@
         first.append(
             push(r_buf.at[cut(to * cap, cap), :], piece(me, place), e_send.at[i], e_recv.at[i], others[i - 1])
         )
+    for i in range(1, ne):
+        to = lax.rem(place + i, ne)
+        scales.append(
+            push(
+                gain_ref.at[pl.ds(kind(to), 1), :], gains.at[:, cut(place * width, width)],
+                n_send.at[i], n_recv.at[i], others[i - 1],
+            )
+        )
     hops = {}
-    for t in range(n // 2):
-        for i in range(ne):
+    last = n // 2 - 1
+
+    def turn_ring(slices, t):
+        for i in slices:
             if t == 0:
                 local.wait() if i == 0 else first[i - 1].wait_recv()
             for d in range(2):
                 if t:
                     hops[i, d, t - 1].wait_recv()
-                if t == n // 2 - 1 and i % 2 != d:
+                if t == last and i % 2 != d:
                     continue
                 seq_at = ring_device(lax.rem(pos + n + t * (ways[1 - d]), n), n)
                 part = piece(seq_at, lax.rem(place + ne - i, ne))
                 at = (i * 2 + d) * (n // 2) + t
                 hops[i, d, t] = push(part, part, s_send.at[at], s_recv.at[at], nexts[d])
-        if t == 0:
-            for i in range(1, ne):
-                to = lax.rem(place + i, ne)
-                scales.append(
-                    push(
-                        gain_ref.at[pl.ds(kind(to), 1), :], gains.at[:, cut(place * width, width)],
-                        n_send.at[i], n_recv.at[i], others[i - 1],
-                    )
-                )
+
+    def finish_ring(slices):
+        for i in slices:
+            hops[i, i % 2, last].wait_recv()
+
+    depth = ne * width
+    block = depth // n
+    per = n // ne
+    gate_sum[...] = jnp.zeros_like(gate_sum)
+    up_sum[...] = jnp.zeros_like(up_sum)
+    state = [jnp.zeros((count, 1), jnp.float32), jnp.zeros((count, HD), jnp.float32)]
+
+    def expand(i, sub):
+        origin = lax.rem(place + ne - i, ne) * width + sub * block
+        at = cut(origin, block)
+        packed = jnp.dot(pack, rows[:, at], preferred_element_type=jnp.float32)
+        state[0] += jnp.sum(packed * packed, axis=1, keepdims=True)
+        scaled = packed * gains[:, at]
+        scored = scaled * router_ref[:, at].astype(jnp.float32)
+        for r in range(block // HD):
+            state[1] += scored[:, r * HD : (r + 1) * HD]
+        part = scaled.astype(jnp.bfloat16)
+        gate_sum[...] += jnp.dot(part, wg[at, :], preferred_element_type=jnp.float32)
+        up_sum[...] += jnp.dot(part, wu[at, :], preferred_element_type=jnp.float32)
+
+    early, late = range(ne // 2), range(ne // 2, ne)
+    for t in range(n // 2):
+        turn_ring(early, t)
+    turn_ring(late, 0)
     own_gain.wait()
     for copy in scales:
         copy.wait_recv()
-    for i in range(ne):
-        hops[i, i % 2, n // 2 - 1].wait_recv()
-
-    count = pack_ref.shape[0]
-    depth = ne * width
-    square = jnp.zeros((count, 1), jnp.float32)
-    for e in range(ne):
-        span = slice(e * width, (e + 1) * width)
-        packed = jnp.dot(pack_ref[...], rows[:, span], preferred_element_type=jnp.float32)
-        square += jnp.sum(packed * packed, axis=1, keepdims=True)
-        normed[:, span] = packed.astype(jnp.bfloat16)
-    inverse = lax.rsqrt(square / depth + 1e-05)
-    logits = jnp.zeros((count, 1), jnp.float32)
-    for e in range(ne):
-        span = slice(e * width, (e + 1) * width)
-        scaled = (normed[:, span].astype(jnp.float32) * inverse * gains[:, span]).astype(jnp.bfloat16)
-        normed[:, span] = scaled
-        logits += jnp.sum(scaled.astype(jnp.float32) * router_ref[:, span], axis=1, keepdims=True)
-    gate = jax.nn.sigmoid(logits)
-
+    finish_ring(early)
     loads[0].wait()
     loads[1].wait()
-    hidden = wg.shape[1]
-    block = depth // n
-
-    def expand(j, sums):
-        at = cut(j * block, block)
-        part = normed[:, at]
-        return (
-            sums[0] + jnp.dot(part, wg[at, :], preferred_element_type=jnp.float32),
-            sums[1] + jnp.dot(part, wu[at, :], preferred_element_type=jnp.float32),
-        )
-
-    zero = jnp.zeros((count, hidden), jnp.float32)
-    gate_part, up_part = lax.fori_loop(0, n, expand, (zero, zero))
-    inner = (jax.nn.silu(gate_part) * up_part).astype(jnp.bfloat16)
+    for t in range(n // 2):
+        if t:
+            turn_ring(late, t)
+        expand(t // per, t % per)
+    finish_ring(late)
+    for t in range(n // 2):
+        expand(ne // 2 + t // per, t % per)
+    inverse = lax.rsqrt(state[0] / depth + 1e-05)
+    gate = jax.nn.sigmoid(inverse * jnp.sum(state[1], axis=1, keepdims=True))
+    inner = (jax.nn.silu(inverse * gate_sum[...]) * (inverse * up_sum[...])).astype(jnp.bfloat16)
     loads[2].wait()
 
     def partial(k, side):
@@ -431,9 +468,8 @@
         sent[k - 1].wait_recv()
         total += z_buf[k].astype(jnp.float32)
     weighted = (gate * total).astype(jnp.bfloat16)
-    w_buf[...] = jnp.dot(unpack_ref[...], weighted, preferred_element_type=jnp.float32).astype(jnp.bfloat16)
-
-    per = n // ne
+    w_buf[...] = crossed(pack, weighted).astype(jnp.bfloat16)
+
     target = me // per
     turn = lax.rem(me, per)
 
@@ -489,34 +525,36 @@
         copy.wait_send()
 
 
-def run_experts(hidden_state, pick_rows, pack, unpack, norm_gain, router_row, w_gate, w_up, w_down, n, ne):
-    count, slots = pack.shape
-    cap = slots // n
-    width = hidden_state.shape[1]
+def run_experts(hidden_state, picks, norm_gain, router, w_gate, w_up, w_down, n, ne, cap):
+    tokens, width = hidden_state.shape
+    count, slots = picks.shape[1], n * cap
     depth, hidden = w_gate.shape
     nz, block = n // 2, depth // n
     bf, f32 = jnp.bfloat16, jnp.float32
     inside = pl.BlockSpec(memory_space=pltpu.VMEM)
-    anywhere = pl.BlockSpec(memory_space=pl.ANY)
+    outside = pl.BlockSpec(memory_space=pltpu.HBM)
     slab = pltpu.VMEM((nz, count, block), bf)
     sems = lambda size: pltpu.SemaphoreType.DMA((size,))
     return pl.pallas_call(
         functools.partial(experts_kernel, n, ne, cap),
-        out_shape=jax.ShapeDtypeStruct((ne * cap, width), bf),
-        in_specs=[inside] * 6 + [anywhere] * 3,
-        out_specs=anywhere,
+        out_shape=(
+            jax.ShapeDtypeStruct((ne * cap, width), bf),
+            jax.ShapeDtypeStruct((ne * cap, tokens), bf),
+        ),
+        in_specs=[inside] * 4 + [outside] * 3,
+        out_specs=(outside, inside),
         scratch_shapes=[
             pltpu.VMEM((depth, hidden), bf), pltpu.VMEM((depth, hidden), bf), pltpu.VMEM((hidden, depth), bf),
             pltpu.VMEM((ne * cap, width), bf), pltpu.VMEM((slots, depth), bf), pltpu.VMEM((1, depth), f32),
-            pltpu.VMEM((count, depth), bf), pltpu.VMEM((nz, count, block), f32),
+            pltpu.VMEM((count, hidden), f32), pltpu.VMEM((count, hidden), f32), pltpu.VMEM((nz, count, block), f32),
             slab, slab, slab, slab, pltpu.VMEM((slots, block), bf),
             sems(3), sems(ne), sems(ne), sems(ne), sems(ne), sems(ne * n), sems(ne * n),
             sems(nz), sems(nz), sems(nz), sems(nz), sems(n), sems(n), sems(3),
         ],
         compiler_params=pltpu.CompilerParams(
-            collective_id=2, has_side_effects=True, vmem_limit_bytes=56 * 1024 * 1024
+            collective_id=2, has_side_effects=True, vmem_limit_bytes=44 * 1024 * 1024
         ),
-    )(hidden_state, pick_rows, pack, unpack, norm_gain, router_row, w_gate, w_up, w_down)
+    )(hidden_state, picks, norm_gain, router.reshape(1, -1), w_gate, w_up, w_down)
 
 
 def flash_kernel(block, border_ref, q_ref, k_ref, v_ref, o_ref):
@@ -1004,7 +1042,7 @@
         + [sems(3 * group)] * 3 + [sems(steps)] * 12 + [sems(group)] * 2 + [sems(steps)] * 6
         + [pltpu.SemaphoreType.DMA((steps, n_exp)), pltpu.SemaphoreType.DMA(())],
         compiler_params=pltpu.CompilerParams(
-            collective_id=0, has_side_effects=True, vmem_limit_bytes=60 * 1024 * 1024
+            collective_id=0, has_side_effects=True, vmem_limit_bytes=54 * 1024 * 1024
         ),
     )(documents.reshape(-1, HD), queries, keys, values, residual, out_proj)
 
@@ -1116,32 +1154,13 @@
         attended = attend_by_token(queries, keys, values, documents)
         mixed = jnp.dot(attended, out_proj, preferred_element_type=jnp.float32)
         hidden_state = (residual.astype(jnp.float32) + mixed).astype(jnp.bfloat16)
-    hidden_wide = hidden_state.astype(jnp.float32)
-    capacity = tokens // 32
-    inside = (picks >= start_row) & (picks < start_row + tokens)
-    slot_index = jnp.cumsum(inside.astype(jnp.int32), axis=1) - 1
-    matched = inside[:, None, :] & (
-        slot_index[:, None, :] == jnp.arange(capacity, dtype=jnp.int32)[None, :, None]
+    returned, placing = run_experts(
+        hidden_state, picks, norm_gain, router, w_gate[0], w_up[0], w_down[0], n_seq, n_exp, tokens // 32
     )
-    local_index = jnp.sum(jnp.where(matched, picks[:, None, :] - start_row, 0), axis=2)
-    filled = jnp.any(matched, axis=2)
-    placing = (
-        (jnp.arange(tokens, dtype=jnp.int32)[:, None] == local_index.reshape(1, -1))
-        & filled.reshape(1, -1)
-    ).astype(jnp.bfloat16)
-    picked = lax.dynamic_index_in_dim(picks, lax.axis_index("exp"), 0, keepdims=False)
-    home = picked // tokens
-    rank = jnp.arange(picked.shape[0], dtype=jnp.int32) - jnp.sum(
-        (home[None, :] < home[:, None]).astype(jnp.int32), axis=1
+    expert_add = lax.dot_general(
+        placing, returned, (((0,), (0,)), ((), ())), preferred_element_type=jnp.float32
     )
-    slot = home * capacity + rank
-    pack = (slot[:, None] == jnp.arange(n_seq * capacity, dtype=jnp.int32)[None, :]).astype(jnp.bfloat16)
-    returned = run_experts(
-        hidden_state, placing.T, pack, pack.T, norm_gain, router.astype(jnp.float32).reshape(1, -1),
-        w_gate[0], w_up[0], w_down[0], n_seq, n_exp,
-    )
-    expert_add = jnp.dot(placing, returned, preferred_element_type=jnp.float32)
-    return (hidden_wide + expert_add).astype(jnp.bfloat16)
+    return (hidden_state.astype(jnp.float32) + expert_add).astype(jnp.bfloat16)
 
 
 def solution(mesh):

time: 155 us -> 147 us (0.948)
  other arithmetic: 7.6 us -> 0 us
    convert_element_type x4 -> x0, other arithmetic: 2.71 us -> none  [the longest x2 1.3 us: shards(): (slot[:, None] == jnp.arange(n_seq * capacity, dtype=jnp.int32)[None, :])...]
    unnamed x2 -> x8, local copies, waits for them, and re-layouts: 0.01 us -> 1.6 us
where the time goes in v4:
time: 147 us; the launch traced here: 146 us
  Pallas kernels  143 us (97%)
  matrix products  2.05 us (1%)
  local copies, waits for them, and re-layouts  1.6 us (1%)
    pallas_call x1, Pallas kernels, attend_by_chain(): pl.pallas_call(functools.partial(chain_kernel, nz, n_exp, group), out_sha...  78.1 us
    pallas_call x1, Pallas kernels, run_experts(): pl.pallas_call(functools.partial(experts_kernel, n, ne, cap), out_shape=(...  64.6 us

profile of v4, /device:TPU:5, one launch (start us, length us, event | category | flops | bytes accessed | tf_op | source)
XLA Modules:
  0.0 146.4 jit_solution(9519630194904211040)
XLA Ops:
  0.0 0.0 copy-start.1
  0.0 0.0 copy-start.2
  0.0 0.0 copy-start.3
  0.0 78.1 %shard_map.118.hid_ref = bf16[512,2048]{1,0:T(8,128)(2,1)} custom-call(s32[32,128]{1,0:T(8,128)} %bitcast.11, bf16[512,1024]{1,0:T(8,128)(2,1)} %q_ref.1, bf16[512,1024]{1,0:T(8,128)(2,1)} %k_ref.1, bf16[512,1024]{1,0:T(8,128)(2,1)} %v_ref.1, bf16[512,2048]{1,0:T(8,128)(2,1)} %res_ref.1, bf16[4096,2048]{1,0:T(8,128)(2,1)} %w_ref.1), custom_call_target="tpu_custom_call" | custom-call | tf_op jit(solution)/shard_map/pallas_call | solution.py:1033
  78.1 0.0 copy-done.1
  78.1 0.0 copy-done.2
  78.1 0.0 copy-done.3
  78.1 0.0 copy-start
  78.1 1.6 %copy-done = bf16[512,2048]{1,0:T(8,128)(2,1)S(1)} copy-done((bf16[512,2048]{1,0:T(8,128)(2,1)S(1)}, bf16[512,2048]{1,0:T(8,128)(2,1)}, u32[]{:S(2)}) %copy-start) | copy-done | bytes 2097176
  79.7 64.6 %shard_map.119 = (bf16[64,2048]{1,0:T(8,128)(2,1)S(1)}, bf16[64,512]{1,0:T(8,128)(2,1)S(1)}) custom-call(bf16[512,2048]{1,0:T(8,128)(2,1)S(1)} %copy-done, s32[4,64]{1,0:T(4,128)S(1)} %copy-done.3, f32[2,2048]{1,0:T(2,128)S(1)} %copy-done.2, bf16[1,8192]{1,0:T(2,128)(2,1)S(1)} %bitcast.7, bf16[8192,512]{1,0:T(8,128)(2,1)} %bitcast.8, ...), custom_call_target="tpu_custom_call" | custom-call | tf_op jit(solution)/shard_map/pallas_call | solution.py:538
  144.3 2.0 %add_convert_fusion = bf16[512,2048]{1,0:T(8,128)(2,1)} fusion(bf16[512,2048]{1,0:T(8,128)(2,1)S(1)} %copy-done, bf16[64,512]{1,0:T(8,128)(2,1)S(1)} %get-tuple-element.7, bf16[64,2048]{1,0:T(8,128)(2,1)S(1)} %get-tuple-element.8), kind=kOutput, calls=%fused_computation | convolution fusion | flops 137363456 | bytes 4521984 | tf_op jit(solution)/shard_map/dot_general | solution.py:1160
Async XLA Ops:
  0.0 78.1 %copy-start.1 = (bf16[8192,1]{0,1:T(2,128)(2,1)S(1)}, bf16[8192,1]{0,1:T(2,128)(2,1)}, u32[]{:S(2)}) copy-start(bf16[8192,1]{0,1:T(2,128)(2,1)} %param.21) | copy-start | bytes 49156
  0.0 78.1 %copy-start.2 = (f32[2,2048]{1,0:T(2,128)S(1)}, f32[2,2048]{1,0:T(2,128)}, u32[]{:S(2)}) copy-start(f32[2,2048]{1,0:T(2,128)} %gain_ref.1) | copy-start | bytes 49156
  0.0 78.1 %copy-start.3 = (s32[4,64]{1,0:T(4,128)S(1)}, s32[4,64]{1,0:T(4,128)}, u32[]{:S(2)}) copy-start(s32[4,64]{1,0:T(4,128)} %pick_ref.1) | copy-start | bytes 3076
  78.1 1.6 %copy-start = (bf16[512,2048]{1,0:T(8,128)(2,1)S(1)}, bf16[512,2048]{1,0:T(8,128)(2,1)}, u32[]{:S(2)}) copy-start(bf16[512,2048]{1,0:T(8,128)(2,1)} %shard_map.118.hid_ref) | copy-start | bytes 6291460

commit v5 on v4

--- a/solution.py
+++ b/solution.py
@@ -290,8 +290,8 @@
 
 def experts_kernel(
     n, ne, cap, hid_ref, pick_ref, gain_ref, router_ref, wg_ref, wu_ref, wd_ref, o_ref, place_ref,
-    wg, wu, wd, r_buf, rows, gains, gate_sum, up_sum, mine, p_buf, x_buf, s_buf, z_buf, w_buf,
-    w_sem, e_send, e_recv, n_send, n_recv, s_send, s_recv, x_send, x_recv, z_send, z_recv,
+    wg, wu, wd, r_buf, slots, packed, gains, gate_sum, up_sum, mine, p_buf, x_buf, s_buf, z_buf, w_buf,
+    w_sem, a_send, a_recv, n_send, n_recv, s_send, s_recv, x_send, x_recv, z_send, z_recv,
     t_send, t_recv, own,
 ):
     me = lax.axis_index("seq")
@@ -356,25 +356,68 @@
     width = r_buf.shape[1]
     pl.semaphore_wait(barrier, everyone - 1)
 
-    def piece(seq_at, exp_at):
-        return rows.at[cut(seq_at * cap, cap), cut(exp_at * width, width)]
-
     def kind(e):
         return (2 * e) // ne
 
-    local = pltpu.make_async_copy(r_buf.at[cut(place * cap, cap), :], piece(me, place), own.at[0])
-    local.start()
+    depth = ne * width
+    block = depth // n
+    per = n // ne
+    target = me // per
+    turn = lax.rem(me, per)
+    stays = target == place
+
+    sub = max(HD, width // n)
+    share = width // sub
+    groups = depth // (sub * n)
+
+    def hand(k, e):
+        number = place * share + k
+        group = number // n
+        return pltpu.make_async_remote_copy(
+            src_ref=r_buf.at[e * cap : (e + 1) * cap, k * sub : (k + 1) * sub],
+            dst_ref=slots.at[cut(me * cap, cap), cut(group * sub, sub)],
+            send_sem=a_send.at[k * ne + e], recv_sem=a_recv.at[me * groups + group],
+            device_id={"seq": lax.rem(number, n), "exp": e}, device_id_type=MESH,
+        )
+
+    def given(at, group):
+        spot = slots.at[at * cap : (at + 1) * cap, group * sub : (group + 1) * sub]
+        return pltpu.make_async_remote_copy(
+            src_ref=spot, dst_ref=spot, send_sem=a_send.at[0], recv_sem=a_recv.at[at * groups + group],
+            device_id=partner, device_id_type=MESH,
+        )
+
+    def to_self(k, e):
+        return stays & (turn == k) & (place == e)
+
+    def hand_self(k, e):
+        return (lax.rem(place * share + k, n) == me) & (place == e)
+
+    def kept(k, e):
+        group = (place * share + k) // n
+        return pltpu.make_async_copy(
+            r_buf.at[e * cap : (e + 1) * cap, k * sub : (k + 1) * sub],
+            slots.at[cut(me * cap, cap), cut(group * sub, sub)],
+            own.at[0],
+        )
+
+    for k in range(share):
+        for e in range(ne):
+            handed, held = hand(k, e), kept(k, e)
+
+            @pl.when(jnp.logical_not(hand_self(k, e)))
+            def _():
+                handed.start()
+
+            @pl.when(hand_self(k, e))
+            def _():
+                held.start()
+
     own_gain = pltpu.make_async_copy(
         gain_ref.at[pl.ds(kind(place), 1), :], gains.at[:, cut(place * width, width)], own.at[1]
     )
     own_gain.start()
-    first = []
     scales = []
-    for i in range(1, ne):
-        to = lax.rem(place + i, ne)
-        first.append(
-            push(r_buf.at[cut(to * cap, cap), :], piece(me, place), e_send.at[i], e_recv.at[i], others[i - 1])
-        )
     for i in range(1, ne):
         to = lax.rem(place + i, ne)
         scales.append(
@@ -383,64 +426,68 @@
                 n_send.at[i], n_recv.at[i], others[i - 1],
             )
         )
+    first_own = place * share
+    for at in range(n):
+        for group in range(groups):
+            arrived = given(at, group)
+            from_self = (me == at) & (first_own <= group * n + me) & (group * n + me < first_own + share)
+
+            @pl.when(jnp.logical_not(from_self))
+            def _():
+                arrived.wait_recv()
+
+    for k in range(share):
+        for e in range(ne):
+            held = kept(k, e)
+
+            @pl.when(hand_self(k, e))
+            def _():
+                held.wait()
+
+    packed[me] = jnp.dot(pack, slots[...], preferred_element_type=jnp.float32).astype(jnp.bfloat16)
+    pieces = 4
+    lines_at = count // pieces
+    gate_sum[...] = jnp.zeros_like(gate_sum)
+    up_sum[...] = jnp.zeros_like(up_sum)
+    state = [jnp.zeros((count, 1), jnp.float32), jnp.zeros((count, HD), jnp.float32)]
+
+    def expand(seq_at):
+        for group in range(groups):
+            at = cut((group * n + seq_at) * sub, sub)
+            raw = packed[seq_at, :, group * sub : (group + 1) * sub].astype(jnp.float32)
+            state[0] += jnp.sum(raw * raw, axis=1, keepdims=True)
+            scaled = raw * gains[:, at]
+            scored = scaled * router_ref[:, at].astype(jnp.float32)
+            for r in range(sub // HD):
+                state[1] += scored[:, r * HD : (r + 1) * HD]
+            part = scaled.astype(jnp.bfloat16)
+            gate_sum[...] += jnp.dot(part, wg[at, :], preferred_element_type=jnp.float32)
+            up_sum[...] += jnp.dot(part, wu[at, :], preferred_element_type=jnp.float32)
+
     hops = {}
     last = n // 2 - 1
-
-    def turn_ring(slices, t):
-        for i in slices:
-            if t == 0:
-                local.wait() if i == 0 else first[i - 1].wait_recv()
+    for t in range(n // 2):
+        arrived_at = [ring_device(lax.rem(pos + n + t * ways[1 - d], n), n) for d in range(2)]
+        for i in range(pieces):
             for d in range(2):
                 if t:
                     hops[i, d, t - 1].wait_recv()
                 if t == last and i % 2 != d:
                     continue
-                seq_at = ring_device(lax.rem(pos + n + t * (ways[1 - d]), n), n)
-                part = piece(seq_at, lax.rem(place + ne - i, ne))
+                part = packed.at[arrived_at[d], i * lines_at : (i + 1) * lines_at, :]
                 at = (i * 2 + d) * (n // 2) + t
                 hops[i, d, t] = push(part, part, s_send.at[at], s_recv.at[at], nexts[d])
-
-    def finish_ring(slices):
-        for i in slices:
-            hops[i, i % 2, last].wait_recv()
-
-    depth = ne * width
-    block = depth // n
-    per = n // ne
-    gate_sum[...] = jnp.zeros_like(gate_sum)
-    up_sum[...] = jnp.zeros_like(up_sum)
-    state = [jnp.zeros((count, 1), jnp.float32), jnp.zeros((count, HD), jnp.float32)]
-
-    def expand(i, sub):
-        origin = lax.rem(place + ne - i, ne) * width + sub * block
-        at = cut(origin, block)
-        packed = jnp.dot(pack, rows[:, at], preferred_element_type=jnp.float32)
-        state[0] += jnp.sum(packed * packed, axis=1, keepdims=True)
-        scaled = packed * gains[:, at]
-        scored = scaled * router_ref[:, at].astype(jnp.float32)
-        for r in range(block // HD):
-            state[1] += scored[:, r * HD : (r + 1) * HD]
-        part = scaled.astype(jnp.bfloat16)
-        gate_sum[...] += jnp.dot(part, wg[at, :], preferred_element_type=jnp.float32)
-        up_sum[...] += jnp.dot(part, wu[at, :], preferred_element_type=jnp.float32)
-
-    early, late = range(ne // 2), range(ne // 2, ne)
-    for t in range(n // 2):
-        turn_ring(early, t)
-    turn_ring(late, 0)
-    own_gain.wait()
-    for copy in scales:
-        copy.wait_recv()
-    finish_ring(early)
-    loads[0].wait()
-    loads[1].wait()
-    for t in range(n // 2):
-        if t:
-            turn_ring(late, t)
-        expand(t // per, t % per)
-    finish_ring(late)
-    for t in range(n // 2):
-        expand(ne // 2 + t // per, t % per)
+        if t == 0:
+            own_gain.wait()
+            for copy in scales:
+                copy.wait_recv()
+            loads[0].wait()
+            loads[1].wait()
+        for d in range(2 if t else 1):
+            expand(arrived_at[d])
+    for i in range(pieces):
+        hops[i, i % 2, last].wait_recv()
+    expand(ring_device(lax.rem(pos + n // 2, n), n))
     inverse = lax.rsqrt(state[0] / depth + 1e-05)
     gate = jax.nn.sigmoid(inverse * jnp.sum(state[1], axis=1, keepdims=True))
     inner = (jax.nn.silu(inverse * gate_sum[...]) * (inverse * up_sum[...])).astype(jnp.bfloat16)
@@ -470,9 +517,6 @@
     weighted = (gate * total).astype(jnp.bfloat16)
     w_buf[...] = crossed(pack, weighted).astype(jnp.bfloat16)
 
-    target = me // per
-    turn = lax.rem(me, per)
-
     def deliver(i):
         to = lax.rem(me + i, n)
         at = turn * ne + place
@@ -486,7 +530,6 @@
     home = pltpu.make_async_copy(
         w_buf.at[cut(me * cap, cap), :], o_ref.at[cut(place * cap, cap), cut(turn * block, block)], own.at[2]
     )
-    stays = target == place
     for i in range(1, n):
         deliver(i).start()
 
@@ -507,7 +550,7 @@
                 device_id=partner, device_id_type=MESH,
             )
 
-            @pl.when(jnp.logical_not(stays & (turn == k) & (place == e)))
+            @pl.when(jnp.logical_not(to_self(k, e)))
             def _():
                 arrival.wait_recv()
 
@@ -521,7 +564,15 @@
 
     for i in range(1, n):
         deliver(i).wait_send()
-    for copy in first + scales + list(hops.values()) + list(pairs.values()) + sent:
+    for k in range(share):
+        for e in range(ne):
+            handed = hand(k, e)
+
+            @pl.when(jnp.logical_not(hand_self(k, e)))
+            def _():
+                handed.wait_send()
+
+    for copy in scales + list(hops.values()) + list(pairs.values()) + sent:
         copy.wait_send()
 
 
@@ -545,10 +596,11 @@
         out_specs=(outside, inside),
         scratch_shapes=[
             pltpu.VMEM((depth, hidden), bf), pltpu.VMEM((depth, hidden), bf), pltpu.VMEM((hidden, depth), bf),
-            pltpu.VMEM((ne * cap, width), bf), pltpu.VMEM((slots, depth), bf), pltpu.VMEM((1, depth), f32),
+            pltpu.VMEM((ne * cap, width), bf), pltpu.VMEM((slots, block), bf),
+            pltpu.VMEM((n, count, block), bf), pltpu.VMEM((1, depth), f32),
             pltpu.VMEM((count, hidden), f32), pltpu.VMEM((count, hidden), f32), pltpu.VMEM((nz, count, block), f32),
             slab, slab, slab, slab, pltpu.VMEM((slots, block), bf),
-            sems(3), sems(ne), sems(ne), sems(ne), sems(ne), sems(ne * n), sems(ne * n),
+            sems(3), sems(ne * n), sems(ne * n), sems(ne), sems(ne), sems(4 * n), sems(4 * n),
             sems(nz), sems(nz), sems(nz), sems(nz), sems(n), sems(n), sems(3),
         ],
         compiler_params=pltpu.CompilerParams(

time: 147 us -> 140 us (0.952)
  Pallas kernels: 143 us -> 136 us
    pallas_call x1, Pallas kernels: 64.6 us -> 57.8 us  [run_experts(): pl.pallas_call(functools.partial(experts_kernel, n, ne, cap), out_shape=(...]
where the time goes in v5:
time: 140 us
  Pallas kernels  136 us (97%)
  matrix products  2.05 us (1%)
  local copies, waits for them, and re-layouts  1.6 us (1%)
    pallas_call x1, Pallas kernels, attend_by_chain(): pl.pallas_call(functools.partial(chain_kernel, nz, n_exp, group), out_sha...  78.1 us
    pallas_call x1, Pallas kernels, run_experts(): pl.pallas_call(functools.partial(experts_kernel, n, ne, cap), out_shape=(...  57.8 us

profile of v5, /device:TPU:5, one launch (start us, length us, event | category | flops | bytes accessed | tf_op | source)
XLA Modules:
  0.0 139.5 jit_solution(8593507878009169953)
XLA Ops:
  0.0 0.0 copy-start.1
  0.0 0.0 copy-start.2
  0.0 0.0 copy-start.3
  0.0 78.1 %shard_map.118.hid_ref = bf16[512,2048]{1,0:T(8,128)(2,1)} custom-call(s32[32,128]{1,0:T(8,128)} %bitcast.11, bf16[512,1024]{1,0:T(8,128)(2,1)} %q_ref.1, bf16[512,1024]{1,0:T(8,128)(2,1)} %k_ref.1, bf16[512,1024]{1,0:T(8,128)(2,1)} %v_ref.1, bf16[512,2048]{1,0:T(8,128)(2,1)} %res_ref.1, bf16[4096,2048]{1,0:T(8,128)(2,1)} %w_ref.1), custom_call_target="tpu_custom_call" | custom-call | tf_op jit(solution)/shard_map/pallas_call | solution.py:1085
  78.1 0.0 copy-done.1
  78.1 0.0 copy-done.2
  78.1 0.0 copy-done.3
  78.1 0.0 copy-start
  78.1 1.6 %copy-done = bf16[512,2048]{1,0:T(8,128)(2,1)S(1)} copy-done((bf16[512,2048]{1,0:T(8,128)(2,1)S(1)}, bf16[512,2048]{1,0:T(8,128)(2,1)}, u32[]{:S(2)}) %copy-start) | copy-done | bytes 2097176
  79.7 57.8 %shard_map.119 = (bf16[64,2048]{1,0:T(8,128)(2,1)S(1)}, bf16[64,512]{1,0:T(8,128)(2,1)S(1)}) custom-call(bf16[512,2048]{1,0:T(8,128)(2,1)S(1)} %copy-done, s32[4,64]{1,0:T(4,128)S(1)} %copy-done.3, f32[2,2048]{1,0:T(2,128)S(1)} %copy-done.2, bf16[1,8192]{1,0:T(2,128)(2,1)S(1)} %bitcast.7, bf16[8192,512]{1,0:T(8,128)(2,1)} %bitcast.8, ...), custom_call_target="tpu_custom_call" | custom-call | tf_op jit(solution)/shard_map/pallas_call | solution.py:589
  137.5 2.0 %add_convert_fusion = bf16[512,2048]{1,0:T(8,128)(2,1)} fusion(bf16[512,2048]{1,0:T(8,128)(2,1)S(1)} %copy-done, bf16[64,512]{1,0:T(8,128)(2,1)S(1)} %get-tuple-element.7, bf16[64,2048]{1,0:T(8,128)(2,1)S(1)} %get-tuple-element.8), kind=kOutput, calls=%fused_computation | convolution fusion | flops 137363456 | bytes 4521984 | tf_op jit(solution)/shard_map/dot_general | solution.py:1212
Async XLA Ops:
  0.0 78.1 %copy-start.1 = (bf16[8192,1]{0,1:T(2,128)(2,1)S(1)}, bf16[8192,1]{0,1:T(2,128)(2,1)}, u32[]{:S(2)}) copy-start(bf16[8192,1]{0,1:T(2,128)(2,1)} %param.21) | copy-start | bytes 49156
  0.0 78.1 %copy-start.2 = (f32[2,2048]{1,0:T(2,128)S(1)}, f32[2,2048]{1,0:T(2,128)}, u32[]{:S(2)}) copy-start(f32[2,2048]{1,0:T(2,128)} %gain_ref.1) | copy-start | bytes 49156
  0.0 78.1 %copy-start.3 = (s32[4,64]{1,0:T(4,128)S(1)}, s32[4,64]{1,0:T(4,128)}, u32[]{:S(2)}) copy-start(s32[4,64]{1,0:T(4,128)} %pick_ref.1) | copy-start | bytes 3076
  78.1 1.6 %copy-start = (bf16[512,2048]{1,0:T(8,128)(2,1)S(1)}, bf16[512,2048]{1,0:T(8,128)(2,1)}, u32[]{:S(2)}) copy-start(bf16[512,2048]{1,0:T(8,128)(2,1)} %shard_map.118.hid_ref) | copy-start | bytes 6291460

commit v6 on v5

--- a/solution.py
+++ b/solution.py
@@ -682,9 +682,9 @@
 
 def chain_kernel(
     nz, ne, group, docs_ref, q_ref, k_ref, v_ref, res_ref, w_ref, o_ref,
-    q0, q1, q2, kb, vb, o0, o1, c0, c1, s2, s1, p2, p1, ls2, ls1, lp2, lp1, back, att, proj, acc, res,
-    load, x_send, x_recv, d0_send, d0_recv, d1_send, d1_recv, u2_send, u2_recv, g2_send, g2_recv,
-    u1_send, u1_recv, g1_send, g1_recv, b_send, b_recv, y_send, y_recv, m_send, m_recv,
+    q0, q1, q2, kb, vb, o0, o1, c0, c1, s2, s1, p2, p1, back, att, proj, acc, res,
+    load, x_send, x_recv, d0_send, d0_recv, d1_send, d1_recv, u2_send, u2_recv,
+    u1_send, u1_recv, b_send, b_recv, y_send, y_recv, m_send, m_recv,
     r_send, r_recv, w_sem, res_sem,
 ):
     me = lax.axis_index("seq")
@@ -743,13 +743,11 @@
     def part2_up(t):
         return (
             remote(s2.at[t], p2.at[t], u2_send.at[t], u2_recv.at[t], up),
-            remote(ls2.at[t], lp2.at[t], g2_send.at[t], g2_recv.at[t], up),
         )
 
     def part1_up(t):
         return (
             remote(s1.at[t], p1.at[t], u1_send.at[t], u1_recv.at[t], up),
-            remote(ls1.at[t], lp1.at[t], g1_send.at[t], g1_recv.at[t], up),
         )
 
     def spot(at, t):
@@ -829,14 +827,25 @@
                 )
             put(r * big, out / total, top + jnp.log2(total))
 
-    def flat(level):
-        return jnp.sum(jnp.where(diagonal, level, 0.0), axis=0, keepdims=True)
+    lines_at = tokens // tile
+
+    def note(ref, i, row, level):
+        rest = jnp.sum(jnp.where(diagonal, level, 0.0), axis=0, keepdims=True)
+        for k in range(3):
+            at = tokens + k * lines_at + row
+            part = rest.astype(jnp.bfloat16)
+            ref[i, at : at + 1, :] = part
+            rest = rest - part.astype(jnp.float32)
 
     def upright(ref, r):
-        return jnp.sum(jnp.where(diagonal, ref[r : r + 1, :], 0.0), axis=1, keepdims=True)
-
-    def joined(out, level, p_of, l_of, r):
-        other = upright(l_of, r)
+        line = jnp.zeros((1, tile), jnp.float32)
+        for k in range(3):
+            at = tokens + k * lines_at + r
+            line += ref[at : at + 1, :].astype(jnp.float32)
+        return jnp.sum(jnp.where(diagonal, line, 0.0), axis=1, keepdims=True)
+
+    def joined(out, level, p_of, r):
+        other = upright(p_of, r)
         top = jnp.maximum(level, other)
         mine, theirs = jnp.exp2(level - top), jnp.exp2(other - top)
         both = mine + theirs
@@ -910,7 +919,7 @@
                 s2[i, at : at + big, :] = out.astype(jnp.bfloat16)
                 for r in range(big // tile):
                     row = at // tile + r
-                    ls2[i, row : row + 1, :] = flat(level[r * tile : (r + 1) * tile])
+                    note(s2, i, row, level[r * tile : (r + 1) * tile])
 
             attend(q2.at[i], 2, i, put, 2)
             for copy in part2_up(i):
@@ -927,14 +936,14 @@
         def _():
             def put(r, out, level):
                 s1[t1, r * tile : (r + 1) * tile, :] = out.astype(jnp.bfloat16)
-                ls1[t1, r : r + 1, :] = flat(level)
+                note(s1, t1, r, level)
 
             @pl.when(low1)
             def _():
                 for copy in part2_up(t1):
                     copy.wait_recv()
                 for r in range(tiles):
-                    put(r, *joined(o1[t1, r * tile : (r + 1) * tile, :], c1[t1, r * tile : (r + 1) * tile, :], p2.at[t1], lp2.at[t1], r))
+                    put(r, *joined(o1[t1, r * tile : (r + 1) * tile, :], c1[t1, r * tile : (r + 1) * tile, :], p2.at[t1], r))
 
             @pl.when(jnp.logical_not(low1))
             def _():
@@ -962,7 +971,7 @@
                     for copy in part1_up(t0):
                         copy.wait_recv()
                     for r in range(tiles):
-                        out, level = joined(o0[t0, r * tile : (r + 1) * tile, :], c0[t0, r * tile : (r + 1) * tile, :], p1.at[t0], lp1.at[t0], r)
+                        out, level = joined(o0[t0, r * tile : (r + 1) * tile, :], c0[t0, r * tile : (r + 1) * tile, :], p1.at[t0], r)
                         put(r, out)
 
                 @pl.when(jnp.logical_not(low1))
@@ -1080,18 +1089,18 @@
     side = pltpu.VMEM((group, 2 * tokens, HD), bf)
     wide = pltpu.VMEM((steps, tokens, HD), f32)
     thin = pltpu.VMEM((steps, tokens, 1), f32)
-    flats = pltpu.VMEM((steps, max(8, tokens // HD), HD), f32)
+    noted = pltpu.VMEM((steps, tokens + -(-3 * (tokens // HD) // 16) * 16, HD), bf)
     sems = lambda count: pltpu.SemaphoreType.DMA((count,))
     return pl.pallas_call(
         functools.partial(chain_kernel, nz, n_exp, group),
         out_shape=jax.ShapeDtypeStruct((tokens, features), queries.dtype),
         in_specs=[inside] + [outside] * 5,
         out_specs=inside,
-        scratch_shapes=[chunks] * 3 + [side] * 2 + [wide] * 2 + [thin] * 2 + [chunks] * 4 + [flats] * 4
+        scratch_shapes=[chunks] * 3 + [side] * 2 + [wide] * 2 + [thin] * 2 + [noted] * 4
         + [pltpu.VMEM((group, tokens, HD), bf), pltpu.VMEM((steps, tokens, n_exp * HD), bf)]
         + [pltpu.VMEM((steps, n_exp * HD, features), bf), pltpu.VMEM((tokens, features), f32)]
         + [pltpu.VMEM((tokens, features), bf)]
-        + [sems(3 * group)] * 3 + [sems(steps)] * 12 + [sems(group)] * 2 + [sems(steps)] * 6
+        + [sems(3 * group)] * 3 + [sems(steps)] * 8 + [sems(group)] * 2 + [sems(steps)] * 6
         + [pltpu.SemaphoreType.DMA((steps, n_exp)), pltpu.SemaphoreType.DMA(())],
         compiler_params=pltpu.CompilerParams(
             collective_id=0, has_side_effects=True, vmem_limit_bytes=54 * 1024 * 1024

time: 140 us -> 140 us (level)
  no operation moved by 1% of the time
where the time goes in v6:
time: 140 us; the launch traced here: 139 us
  Pallas kernels  136 us (97%)
  matrix products  2.05 us (1%)
  local copies, waits for them, and re-layouts  1.6 us (1%)
    pallas_call x1, Pallas kernels, attend_by_chain(): pl.pallas_call(functools.partial(chain_kernel, nz, n_exp, group), out_sha...  77.8 us
    pallas_call x1, Pallas kernels, run_experts(): pl.pallas_call(functools.partial(experts_kernel, n, ne, cap), out_shape=(...  57.8 us

profile of v6, /device:TPU:5, one launch (start us, length us, event | category | flops | bytes accessed | tf_op | source)
XLA Modules:
  0.0 139.3 jit_solution(11761250775107495276)
XLA Ops:
  0.0 0.0 copy-start.1
  0.0 0.0 copy-start.2
  0.0 0.0 copy-start.3
  0.0 77.8 %shard_map.118.hid_ref = bf16[512,2048]{1,0:T(8,128)(2,1)} custom-call(s32[32,128]{1,0:T(8,128)} %bitcast.11, bf16[512,1024]{1,0:T(8,128)(2,1)} %q_ref.1, bf16[512,1024]{1,0:T(8,128)(2,1)} %k_ref.1, bf16[512,1024]{1,0:T(8,128)(2,1)} %v_ref.1, bf16[512,2048]{1,0:T(8,128)(2,1)} %res_ref.1, bf16[4096,2048]{1,0:T(8,128)(2,1)} %w_ref.1), custom_call_target="tpu_custom_call" | custom-call | tf_op jit(solution)/shard_map/pallas_call | solution.py:1094
  77.8 0.0 copy-done.1
  77.8 0.0 copy-done.2
  77.8 0.0 copy-done.3
  77.8 0.0 copy-start
  77.8 1.6 %copy-done = bf16[512,2048]{1,0:T(8,128)(2,1)S(1)} copy-done((bf16[512,2048]{1,0:T(8,128)(2,1)S(1)}, bf16[512,2048]{1,0:T(8,128)(2,1)}, u32[]{:S(2)}) %copy-start) | copy-done | bytes 2097176
  79.4 57.8 %shard_map.119 = (bf16[64,2048]{1,0:T(8,128)(2,1)S(1)}, bf16[64,512]{1,0:T(8,128)(2,1)S(1)}) custom-call(bf16[512,2048]{1,0:T(8,128)(2,1)S(1)} %copy-done, s32[4,64]{1,0:T(4,128)S(1)} %copy-done.3, f32[2,2048]{1,0:T(2,128)S(1)} %copy-done.2, bf16[1,8192]{1,0:T(2,128)(2,1)S(1)} %bitcast.7, bf16[8192,512]{1,0:T(8,128)(2,1)} %bitcast.8, ...), custom_call_target="tpu_custom_call" | custom-call | tf_op jit(solution)/shard_map/pallas_call | solution.py:589
  137.2 2.1 %add_convert_fusion = bf16[512,2048]{1,0:T(8,128)(2,1)} fusion(bf16[512,2048]{1,0:T(8,128)(2,1)S(1)} %copy-done, bf16[64,512]{1,0:T(8,128)(2,1)S(1)} %get-tuple-element.7, bf16[64,2048]{1,0:T(8,128)(2,1)S(1)} %get-tuple-element.8), kind=kOutput, calls=%fused_computation | convolution fusion | flops 137363456 | bytes 4521984 | tf_op jit(solution)/shard_map/dot_general | solution.py:1221
Async XLA Ops:
  0.0 77.8 %copy-start.1 = (bf16[8192,1]{0,1:T(2,128)(2,1)S(1)}, bf16[8192,1]{0,1:T(2,128)(2,1)}, u32[]{:S(2)}) copy-start(bf16[8192,1]{0,1:T(2,128)(2,1)} %param.21) | copy-start | bytes 49156
  0.0 77.8 %copy-start.2 = (f32[2,2048]{1,0:T(2,128)S(1)}, f32[2,2048]{1,0:T(2,128)}, u32[]{:S(2)}) copy-start(f32[2,2048]{1,0:T(2,128)} %gain_ref.1) | copy-start | bytes 49156
  0.0 77.8 %copy-start.3 = (s32[4,64]{1,0:T(4,128)S(1)}, s32[4,64]{1,0:T(4,128)}, u32[]{:S(2)}) copy-start(s32[4,64]{1,0:T(4,128)} %pick_ref.1) | copy-start | bytes 3076
  77.8 1.6 %copy-start = (bf16[512,2048]{1,0:T(8,128)(2,1)S(1)}, bf16[512,2048]{1,0:T(8,128)(2,1)}, u32[]{:S(2)}) copy-start(bf16[512,2048]{1,0:T(8,128)(2,1)} %shard_map.118.hid_ref) | copy-start | bytes 6291460
